TPU v7x, 1024 devices: a whole 4x8x16 slice. The times are simulated.
1024 devices in a mesh: expert: 16 (over z), dp: 8 (over y), tensor: 8 (over x, core).
Axes of the slice: x: 4, y: 8, z: 16, core: 2. Of those that a mesh axis runs over, the one named last changes fastest.
Arguments:
- tokens: bfloat16 [16384, 4096], P(('expert', 'dp')), may hold values from -6 to 6
- out_grad: bfloat16 [16384, 4096], P(('expert', 'dp')), may hold values from -1.1953125 to 1.1953125
- expert_index: int32 [16384, 2], P(('expert', 'dp')), may hold values from 0 to 15, as said below
- slot_index: int32 [16384, 2], P(('expert', 'dp')), may hold values from 0 to 23, as said below
- gate_probs: float32 [16384, 2], P(('expert', 'dp')), may hold values from 0.05 to 0.95
- gate_weight: bfloat16 [16, 4096, 2048], P('expert', None, 'tensor'), may hold values from -0.09375 to 0.09375
- up_weight: bfloat16 [16, 4096, 2048], P('expert', None, 'tensor'), may hold values from -0.09375 to 0.09375
- down_weight: bfloat16 [16, 2048, 4096], P('expert', 'tensor'), may hold values from -0.125 to 0.125
Outputs:
- token_grad: bfloat16 [16384, 4096], P(('expert', 'dp'), 'tensor')
- gate_grad: bfloat16 [16, 4096, 2048], P('expert', 'dp', 'tensor')
- up_grad: bfloat16 [16, 4096, 2048], P('expert', 'dp', 'tensor')
- down_grad: bfloat16 [16, 2048, 4096], P('expert', 'tensor', 'dp')
Inputs may be any that keep to these rules, and one draw needn't show every extreme that they name: `expert_index`: in each block of 128 rows (the rows of one device) the two experts of a row differ; in every block one expert is named by exactly 24 rows and no expert by more, and that expert is the same for all blocks of one group. `slot_index`: within one block, the choices that name one expert carry distinct slots that run from 0 to their number minus one; a choice whose slot is 12 or more is dropped.
All inputs are finite; a program needn't handle non-finite values.
Results may differ from a plain program's by a relative error of at most 0.014.
Values may be sent and summed in bfloat16 or wider, within the bound.
No kernel may reach another device: no remote copies, remote signals or barrier semaphores. Data moves between devices by JAX's collectives and lax.ppermute only.
A program may use at most 64 MiB of HBM per device.

v0:
```python
import jax
import jax.numpy as jnp
from jax import lax
from jax.experimental import pallas as pl
from jax.experimental.pallas import tpu as pltpu
from jax.sharding import PartitionSpec as P


BF = jnp.bfloat16
F32 = jnp.float32
VM = pl.BlockSpec(memory_space=pltpu.VMEM)
HB = pl.BlockSpec(memory_space=pltpu.HBM)
SM = pl.BlockSpec(memory_space=pltpu.SMEM)
LAST = (((1,), (1,)), ((), ()))
FIRST = (((0,), (0,)), ((), ()))
TENSOR = 8
SIDE = [(t, (t + (2 if t % 2 == 0 else -2)) % TENSOR) for t in range(TENSOR)]
FAR = [(t, (t + 4) % TENSOR) for t in range(TENSOR)]
SWAP = [(t, t ^ 1) for t in range(TENSOR)]


def row_targets(ei, si, q):
    base = ei * 24
    near = base + q * 8 + si
    far = base + 16 + q * 4 + (si - 8)
    return jnp.where(si < 12, jnp.where(si < 8, near, far), -1)


def picks(ei_ref, si_ref, q):
    rows = lax.broadcasted_iota(jnp.int32, (384, 128), 0)
    target = row_targets(ei_ref[...], si_ref[...], q)
    return [rows == target[k : k + 1, :] for k in range(2)]


def far_rows(q):
    row = lax.broadcasted_iota(jnp.int32, (64, 128), 0)
    col = lax.broadcasted_iota(jnp.int32, (64, 128), 1)
    return (col == (row >> 2) * 8 + q * 4 + (row & 3)).astype(BF)


def dispatch_kernel(t_ref, ei_ref, si_ref, prob_ref, tok_hbm, grad_hbm, out_ref, buf, sem):
    t = t_ref[0]
    unit = lax.rem(t, 4)

    def fetch(src):
        for k in range(8):
            q, j = k // 4, k % 4
            pltpu.make_async_copy(
                src.at[:, pl.ds(pl.multiple_of(k * 512 + unit * 128, 128), 128)],
                buf.at[pl.ds(q * 128, 128), pl.ds(j * 128, 128)],
                sem.at[k],
            ).start()
        for k in range(8):
            q, j = k // 4, k % 4
            pltpu.make_async_copy(
                src.at[:, pl.ds(pl.multiple_of(k * 512 + unit * 128, 128), 128)],
                buf.at[pl.ds(q * 128, 128), pl.ds(j * 128, 128)],
                sem.at[k],
            ).wait()

    @pl.when(t < 4)
    def _():
        fetch(tok_hbm)

    @pl.when(t >= 4)
    def _():
        fetch(grad_hbm)

    masks, weight = [], jnp.zeros((384, 1), F32)
    for q in range(2):
        first, second = picks(ei_ref, si_ref, q)
        prob = jnp.where(first, prob_ref[0:1, :], 0.0) + jnp.where(second, prob_ref[1:2, :], 0.0)
        weight = weight + jnp.sum(prob, axis=1, keepdims=True)
        masks.append(jnp.logical_or(first, second).astype(F32).astype(BF))
    rows = jnp.dot(jnp.concatenate(masks, axis=1), buf[...], preferred_element_type=F32)
    weight = jnp.where(t < 4, jnp.ones_like(weight), weight)
    out_ref[...] = (rows * weight).astype(BF)


def unpack(block, q, far):
    near = block[:, q * 8 : (q + 1) * 8, :].reshape(128, block.shape[2])
    rest = block[:, 16:24, :].reshape(128, block.shape[2])
    rest = jnp.dot(far, rest, preferred_element_type=F32).astype(BF)
    return jnp.concatenate([near, rest], axis=0)


def settle(low, high):
    near = low[0:128] + high[0:128]
    width = low.shape[1]
    far = low[128:256].reshape(16, 8, width)
    far = far + pltpu.roll(high[128:256].reshape(16, 8, width), 4, 1)
    pairs = far.reshape(8, 2, 8, width)
    row = lax.broadcasted_iota(jnp.int32, (8, 8, width), 1)
    rest = jnp.where(row < 4, pairs[:, 0], pltpu.roll(pairs[:, 1], 4, 1)).reshape(64, width)
    return jnp.concatenate([near, rest], axis=0)


def forward_kernel(g_hbm, wg_hbm, wu_hbm, wd_hbm, out_ref, buf, wg, wu, wd, sem):
    copies = [pltpu.make_async_copy(g_hbm.at[t], buf.at[t], sem.at[0, t]) for t in range(8)]
    down = [
        pltpu.make_async_copy(
            wd_hbm.at[:, pl.ds(q * 2048, 2048)], wd.at[:, pl.ds(q * 2048, 2048)], sem.at[1, q]
        )
        for q in range(2)
    ]
    first = [
        [
            pltpu.make_async_copy(
                src.at[pl.ds(q * 4, 4)], dst.at[pl.ds(q * 4, 4)], sem.at[2 + side, q]
            )
            for side, (src, dst) in enumerate(((wg_hbm, wg), (wu_hbm, wu)))
        ]
        for q in range(2)
    ]
    for copy in copies[4:8] + down + copies[0:4] + first[0] + first[1]:
        copy.start()

    def rows(units, q):
        return jnp.concatenate(
            [
                jnp.concatenate(
                    [
                        buf[t, :, q * 8 : (q + 1) * 8, :].reshape(128, 512),
                        buf[t, :, 16:24, :].reshape(128, 512),
                    ],
                    axis=0,
                )
                for t in units
            ],
            axis=1,
        )

    for copy in copies[4:8]:
        copy.wait()
    terms = []
    for q in range(2):
        down[q].wait()
        w = jnp.concatenate(
            [
                wd[:, (q * 4 + j) * 512 + unit * 128 : (q * 4 + j) * 512 + (unit + 1) * 128]
                for unit in range(4)
                for j in range(4)
            ],
            axis=1,
        )
        terms.append(
            lax.dot_general(rows(range(4, 8), q), w, LAST, preferred_element_type=F32)
        )
    back = settle(*terms)
    for copy in copies[0:4]:
        copy.wait()
    terms = []
    for q in range(2):
        for copy in first[q]:
            copy.wait()
        w = jnp.concatenate(
            [
                jnp.concatenate(
                    [m[q * 4 : (q + 1) * 4, unit].reshape(512, 256) for unit in range(4)], axis=0
                )
                for m in (wg, wu)
            ],
            axis=1,
        )
        terms.append(jnp.dot(rows(range(4), q), w, preferred_element_type=F32))
    both = settle(*terms)
    gate, up = both[:, 0:256], both[:, 256:512]
    sig = jax.nn.sigmoid(gate)
    act = gate * sig
    out_ref[:, 0:256] = (back * up * sig * (1.0 + gate * (1.0 - sig))).astype(BF)
    out_ref[:, 256:512] = (back * act).astype(BF)
    out_ref[:, 512:768] = (act * up).astype(BF)


def slot_kernel(delta_ref, wg_hbm, wu_hbm, out_ref, wg, wu, sem):
    copies = [
        [
            pltpu.make_async_copy(src.at[k], dst.at[k], sem.at[side, k])
            for side, (src, dst) in enumerate(((wg_hbm, wg), (wu_hbm, wu)))
        ]
        for k in range(8)
    ]
    for group in copies:
        for copy in group:
            copy.start()
    for k in range(8):
        for copy in copies[k]:
            copy.wait()
        w = jnp.concatenate([wg[k].reshape(512, 256), wu[k].reshape(512, 256)], axis=1)
        term = lax.dot_general(delta_ref[:, 0:512], w, LAST, preferred_element_type=F32)
        out_ref[k] = term.astype(BF)


def pack_kernel(parts_ref, out_ref):
    total = parts_ref[0].astype(F32)
    for t in range(1, 8):
        total = total + parts_ref[t].astype(F32)
    rows = total.astype(BF)
    rest = jnp.zeros((128, 256), F32)
    for q in range(2):
        half = rows[:, q * 256 : (q + 1) * 256]
        out_ref[:, q * 8 : (q + 1) * 8, :] = half[0:128].reshape(16, 8, 256)
        rest += lax.dot_general(far_rows(q), half[128:192], FIRST, preferred_element_type=F32)
    out_ref[:, 16:24, :] = rest.astype(BF).reshape(16, 8, 256)


def combine_kernel(ei_ref, si_ref, ret_ref, out_ref):
    for q in range(2):
        first, second = picks(ei_ref, si_ref, q)
        mask = jnp.logical_or(first, second).astype(F32).astype(BF)
        out_ref[:, q * 256 : (q + 1) * 256] = lax.dot_general(
            mask, ret_ref[...], FIRST, preferred_element_type=F32
        ).astype(BF)


def corner_kernel(block_ref, out_ref):
    for q in range(2):
        x = unpack(block_ref[...], q, far_rows(q))
        for j in range(4):
            out_ref[q * 4 + j] = x[:, j * 128 : (j + 1) * 128]


def weight_kernel(t_ref, delta_ref, pair_hbm, side_hbm, side2_hbm, far_hbm, far2_hbm, gate_ref, up_ref, down_ref, buf, sem):
    t = t_ref[0]
    core = lax.rem(t, 2)
    chip = lax.div(t, 2)
    near = jnp.where(core == 0, 3, 1)
    places = [
        (pair_hbm.at[0], 0, core),
        (pair_hbm.at[1], 0, 1 - core),
        (side_hbm.at[0], near, core),
        (side_hbm.at[1], near, 1 - core),
        (side2_hbm.at[0], 4 - near, 1 - core),
        (side2_hbm.at[1], 4 - near, core),
        (far_hbm, 2, core),
        (far2_hbm, 2, 1 - core),
    ]
    copies = [
        pltpu.make_async_copy(src, buf.at[lax.rem(chip + shift, 4) * 2 + which], sem.at[i])
        for i, (src, shift, which) in enumerate(places)
    ]
    for copy in copies:
        copy.start()
    for copy in copies:
        copy.wait()
    tok = jnp.concatenate([buf[u].reshape(1536, 128) for u in range(4)], axis=1)
    both = lax.dot_general(tok, delta_ref[:, 0:512], FIRST, preferred_element_type=F32)
    gate_ref[...] = both[:, 0:256].astype(BF)
    up_ref[...] = both[:, 256:512].astype(BF)
    grad = jnp.concatenate([buf[4 + u].reshape(1536, 128) for u in range(4)], axis=1)
    down_ref[...] = lax.dot_general(
        delta_ref[:, 512:768], grad, FIRST, preferred_element_type=F32
    ).astype(BF)


def call(kernel, out, specs, scratch=(), flops=0, size=0):
    single = not isinstance(out, (list, tuple))
    return pl.pallas_call(
        kernel,
        out_shape=out,
        in_specs=specs,
        out_specs=VM if single else [VM] * len(out),
        scratch_shapes=scratch,
        cost_estimate=pl.CostEstimate(flops=flops, bytes_accessed=size, transcendentals=0),
        compiler_params=pltpu.CompilerParams(vmem_limit_bytes=67_043_328),
    )


def shape(dims, kind=BF):
    return jax.ShapeDtypeStruct(dims, kind)


def layer(tokens, out_grad, expert_index, slot_index, gate_probs, gate_weight, up_weight, down_weight):
    t = lax.axis_index("tensor").astype(jnp.int32).reshape(1)
    ei, si, prob = expert_index.T, slot_index.T, gate_probs.T
    wg = gate_weight.reshape(8, 4, 128, 256)
    wu = up_weight.reshape(8, 4, 128, 256)
    wd = down_weight[0]
    dma = pltpu.SemaphoreType.DMA

    sent = call(
        dispatch_kernel,
        shape((384, 512)),
        [SM, VM, VM, VM, HB, HB],
        [pltpu.VMEM((256, 512), BF), dma((8,))],
        flops=100_000_000,
        size=700_000,
    )(t, ei, si, prob, tokens, out_grad)
    block = lax.all_to_all(sent.reshape(16, 24, 512), "expert", 0, 0, tiled=True)
    whole = lax.all_gather(block.reshape(384, 512), "tensor", axis=0, tiled=True)

    corner = call(
        corner_kernel, shape((8, 192, 128)), [VM], flops=20_000_000, size=800_000
    )(block)
    mine = lax.all_to_all(corner, "dp", 0, 0, tiled=True)
    turned = lax.ppermute(mine, "tensor", SWAP)
    pair = jnp.concatenate([mine[None], turned[None]], axis=0)
    side = lax.ppermute(pair, "tensor", SIDE)
    far = lax.ppermute(mine, "tensor", FAR)
    whole, pair = lax.optimization_barrier((whole, pair))
    delta = call(
        forward_kernel,
        shape((192, 768)),
        [HB, HB, HB, HB],
        [
            pltpu.VMEM((8, 16, 24, 512), BF),
            pltpu.VMEM((8, 4, 128, 256), BF),
            pltpu.VMEM((8, 4, 128, 256), BF),
            pltpu.VMEM((256, 4096), BF),
            dma((4, 8)),
        ],
        flops=1_300_000_000,
        size=10_000_000,
    )(whole.reshape(8, 16, 24, 512), wg, wu, wd)
    side2 = lax.ppermute(side, "tensor", SWAP)
    far2 = lax.ppermute(far, "tensor", SWAP)
    deltas = lax.all_gather(delta, "dp", axis=0, tiled=True)

    terms = call(
        slot_kernel,
        shape((8, 192, 512)),
        [VM, HB, HB],
        [pltpu.VMEM((8, 4, 128, 256), BF), pltpu.VMEM((8, 4, 128, 256), BF), dma((2, 8))],
        flops=800_000_000,
        size=6_000_000,
    )(delta, wg, wu)
    parts = lax.all_to_all(terms, "tensor", 0, 0, tiled=True)
    back = call(pack_kernel, shape((16, 24, 256)), [VM], flops=10_000_000, size=1_800_000)(parts)
    returned = lax.all_to_all(back, "expert", 0, 0, tiled=True)
    gate_grad, up_grad, down_grad = call(
        weight_kernel,
        [shape((512, 256)), shape((512, 256)), shape((256, 512))],
        [SM, VM, HB, HB, HB, HB, HB],
        [pltpu.VMEM((8, 8, 192, 128), BF), dma((8,))],
        flops=1_200_000_000,
        size=6_000_000,
    )(t, deltas, pair, side, side2, far, far2)
    returned, gate_grad = lax.optimization_barrier((returned, gate_grad))
    token_grad = call(
        combine_kernel, shape((128, 512)), [VM, VM, VM], flops=50_000_000, size=400_000
    )(ei, si, returned.reshape(384, 256))
    return (token_grad, gate_grad[None], up_grad[None], down_grad[None])


def solution(mesh):
    rows = P(("expert", "dp"), None)
    return jax.shard_map(
        layer,
        mesh=mesh,
        in_specs=(
            rows,
            rows,
            rows,
            rows,
            rows,
            P("expert", None, "tensor"),
            P("expert", None, "tensor"),
            P("expert", "tensor", None),
        ),
        out_specs=(
            P(("expert", "dp"), "tensor"),
            P("expert", "dp", "tensor"),
            P("expert", "dp", "tensor"),
            P("expert", "tensor", "dp"),
        ),
        check_vma=False,
    )
```

profile of v0, /device:TPU:1, one launch (start us, length us, event | category | flops | bytes accessed | tf_op | source)
XLA Modules:
  0.0 177.3 jit_solution(11063855591576328745)
XLA Ops:
  7.2 0.0 all-gather.3.cloned.1.call-start
  7.2 2.7 %shard_map.111 = bf16[384,512]{1,0:T(8,128)(2,1)} custom-call(s32[1]{0:T(128)} %bitcast.2.t_ref, s32[2,128]{1,0:T(2,128)} %bitcast.25, s32[2,128]{1,0:T(2,128)} %bitcast.27, f32[2,128]{1,0:T(2,128)} %bitcast.29, bf16[128,4096]{1,0:T(8,128)(2,1)} %tok_hbm.1, bf16[128,4096]{1,0:T(8,128)(2,1)} %grad_hbm.1), custom_call_target="tpu_custom_call" | custom-call | flops 100000000 | bytes 700000 | tf_op jit(solution)/shard_map/pallas_call | solution.py:281
  10.0 37.6 %all_to_all.20.block_ref = bf16[16,24,512]{2,1,0:T(8,128)(2,1)} all-to-all(bf16[16,24,512]{2,1,0:T(8,128)(2,1)} %bitcast.23), channel_id=1, replica_groups=mesh['expert'=16,'dp'=8,'tensor'=8] {'expert'}, dimensions={0} | all-to-all | bytes 786432 | tf_op jit(solution)/shard_map/all_to_all | solution.py:289
  47.6 0.0 all-gather.3.cloned.1.call-update
  47.6 0.0 all-gather.5.cloned.1.call-start
  47.7 1.9 %shard_map.112 = bf16[8,192,128]{2,1,0:T(8,128)(2,1)} custom-call(bf16[16,24,512]{2,1,0:T(8,128)(2,1)} %all_to_all.20.block_ref), custom_call_target="tpu_custom_call" | custom-call | flops 20000000 | bytes 800000 | tf_op jit(solution)/shard_map/pallas_call | solution.py:292
  49.6 17.7 %all_to_all.21 = bf16[8,192,128]{2,1,0:T(8,128)(2,1)} all-to-all(bf16[8,192,128]{2,1,0:T(8,128)(2,1)} %shard_map.112), channel_id=1, replica_groups=mesh['expert'=16,'dp'=8,'tensor'=8] {'dp'}, dimensions={0} | all-to-all | bytes 786432 | tf_op jit(solution)/shard_map/all_to_all | solution.py:295
  67.3 10.0 %collective-permute-start = (bf16[8,192,128]{2,1,0:T(8,128)(2,1)}, bf16[8,192,128]{2,1,0:T(8,128)(2,1)S(1)}, u32[]{:S(2)}, u32[]{:S(2)}) collective-permute-start(bf16[8,192,128]{2,1,0:T(8,128)(2,1)} %all_to_all.21), channel_id=1, source_target_pairs={{0,1},{1,0},{2,3},{3,2},{4,5},{5,4},{6,7},{7,6},{8,9},{9,8},{10,11... | collective-permute-start | bytes 1179656 | tf_op jit(solution)/shard_map/ppermute | solution.py:296
  77.2 1.5 collective-permute-done
  78.8 2.0 %pad_maximum_fusion.pair_hbm = bf16[2,8,192,128]{3,2,1,0:T(8,128)(2,1)} fusion(bf16[1,8,192,128]{3,2,1,0:T(8,128)(2,1)S(1)} %bitcast.24, bf16[1,8,192,128]{3,2,1,0:T(8,128)(2,1)} %bitcast.6), kind=kLoop, calls=%fused_computation | loop fusion | flops 393216 | bytes 1572864 | tf_op jit(solution)/shard_map/concatenate | solution.py:297
  80.7 6.6 %all-gather.3.cloned.1.call-done = bf16[3072,512]{1,0:T(8,128)(2,1)} async-done(((bf16[384,512]{1,0:T(8,128)(2,1)}), bf16[3072,512]{1,0:T(8,128)(2,1)}) %all-gather.3.cloned.1.call-update) | async-done | bytes 3145744 | tf_op jit(solution)/shard_map/all_gather | solution.py:290
  87.4 6.2 %shard_map.113.delta_ref = bf16[192,768]{1,0:T(8,128)(2,1)} custom-call(bf16[8,16,24,512]{3,2,1,0:T(8,128)(2,1)} %bitcast.21, bf16[8,4,128,256]{3,2,1,0:T(8,128)(2,1)} %bitcast.16, bf16[8,4,128,256]{3,2,1,0:T(8,128)(2,1)} %bitcast.18, bf16[256,4096]{1,0:T(8,128)(2,1)} %bitcast.22), custom_call_target="tpu_custom_call" | custom-call | flops 1300000000 | bytes 10000000 | tf_op jit(solution)/shard_map/pallas_call | solution.py:301
  93.5 0.0 all-gather.5.cloned.1.call-update
  93.5 5.9 %shard_map.114 = bf16[8,192,512]{2,1,0:T(8,128)(2,1)} custom-call(bf16[192,768]{1,0:T(8,128)(2,1)} %shard_map.113.delta_ref, bf16[8,4,128,256]{3,2,1,0:T(8,128)(2,1)} %bitcast.17, bf16[8,4,128,256]{3,2,1,0:T(8,128)(2,1)} %bitcast.19), custom_call_target="tpu_custom_call" | custom-call | flops 800000000 | bytes 6000000 | tf_op jit(solution)/shard_map/pallas_call | solution.py:319
  99.5 0.0 copy-start
  99.5 4.6 %all-to-all-start.2 = ((bf16[8,192,512]{2,1,0:T(8,128)(2,1)}), bf16[8,192,512]{2,1,0:T(8,128)(2,1)}, u32[]{:S(2)}, u32[]{:S(2)}) async-start(bf16[8,192,512]{2,1,0:T(8,128)(2,1)} %shard_map.114), calls=%async_computation.2 | async-start | bytes 3145728 | tf_op jit(solution)/shard_map/all_to_all | solution.py:327
  104.1 0.0 copy-done
  104.1 4.5 %collective-permute-start.1 = (bf16[2,8,192,128]{3,2,1,0:T(8,128)(2,1)S(1)}, bf16[2,8,192,128]{3,2,1,0:T(8,128)(2,1)}, u32[]{:S(2)}, u32[]{:S(2)}) collective-permute-start(bf16[2,8,192,128]{3,2,1,0:T(8,128)(2,1)S(1)} %copy-done), channel_id=1, source_target_pairs={{0,2},{1,7},{2,4},{3,1},{4,6},{5,3},{6,0},{7,5},{8,10},{9,15},{10,... | collective-permute-start | bytes 2359304 | tf_op jit(solution)/shard_map/ppermute | solution.py:298
  108.6 2.5 %collective-permute-start.3 = (bf16[8,192,128]{2,1,0:T(8,128)(2,1)}, bf16[8,192,128]{2,1,0:T(8,128)(2,1)}, u32[]{:S(2)}, u32[]{:S(2)}) collective-permute-start(bf16[8,192,128]{2,1,0:T(8,128)(2,1)} %all_to_all.21), channel_id=1, source_target_pairs={{0,4},{1,5},{2,6},{3,7},{4,0},{5,1},{6,2},{7,3},{8,12},{9,13},{10,... | collective-permute-start | bytes 1179656 | tf_op jit(solution)/shard_map/ppermute | solution.py:299
  111.1 25.5 %collective-permute-done.1.side_hbm = bf16[2,8,192,128]{3,2,1,0:T(8,128)(2,1)} collective-permute-done((bf16[2,8,192,128]{3,2,1,0:T(8,128)(2,1)S(1)}, bf16[2,8,192,128]{3,2,1,0:T(8,128)(2,1)}, u32[]{:S(2)}, u32[]{:S(2)}) %collective-permute-start.1) | collective-permute-done | bytes 786464 | tf_op jit(solution)/shard_map/ppermute | solution.py:298
  136.5 3.5 %collective-permute-start.2 = (bf16[2,8,192,128]{3,2,1,0:T(8,128)(2,1)}, bf16[2,8,192,128]{3,2,1,0:T(8,128)(2,1)}, u32[]{:S(2)}, u32[]{:S(2)}) collective-permute-start(bf16[2,8,192,128]{3,2,1,0:T(8,128)(2,1)} %collective-permute-done.1.side_hbm), channel_id=1, source_target_pairs={{0,1},{1,0},{2,3},{3,2},{4,5},{5,4},{6,7},{7,6},{8,9},{9,8},{10,11... | collective-permute-start | bytes 2359304 | tf_op jit(solution)/shard_map/ppermute | solution.py:315
  140.0 0.0 all-to-all-done.2.parts_ref
  140.0 2.4 %shard_map.115 = bf16[16,24,256]{2,1,0:T(8,128)(2,1)} custom-call(bf16[8,192,512]{2,1,0:T(8,128)(2,1)} %all-to-all-done.2.parts_ref), custom_call_target="tpu_custom_call" | custom-call | flops 10000000 | bytes 1800000 | tf_op jit(solution)/shard_map/pallas_call | solution.py:328
  142.5 12.8 %all-to-all-start.3 = ((bf16[16,24,256]{2,1,0:T(8,128)(2,1)}), bf16[16,24,256]{2,1,0:T(8,128)(2,1)}, u32[]{:S(2)}, u32[]{:S(2)}) async-start(bf16[16,24,256]{2,1,0:T(8,128)(2,1)} %shard_map.115), calls=%async_computation.3 | async-start | bytes 393216 | tf_op jit(solution)/shard_map/all_to_all | solution.py:329
  155.3 0.0 collective-permute-done.3.far_hbm
  155.3 2.2 %collective-permute-start.4 = (bf16[8,192,128]{2,1,0:T(8,128)(2,1)}, bf16[8,192,128]{2,1,0:T(8,128)(2,1)}, u32[]{:S(2)}, u32[]{:S(2)}) collective-permute-start(bf16[8,192,128]{2,1,0:T(8,128)(2,1)} %collective-permute-done.3.far_hbm), channel_id=1, source_target_pairs={{0,1},{1,0},{2,3},{3,2},{4,5},{5,4},{6,7},{7,6},{8,9},{9,8},{10,11... | collective-permute-start | bytes 1179656 | tf_op jit(solution)/shard_map/ppermute | solution.py:316
  157.5 1.8 collective-permute-done.4.far2_hbm
  159.2 0.0 collective-permute-done.2.side2_hbm
  159.2 0.0 all-gather.5.cloned.1.call-done.delta_ref
  159.2 5.7 %shard_map.116 = (bf16[512,256]{1,0:T(8,128)(2,1)}, bf16[512,256]{1,0:T(8,128)(2,1)}, bf16[256,512]{1,0:T(8,128)(2,1)}) custom-call(s32[1]{0:T(128)} %bitcast.2.t_ref, bf16[1536,768]{1,0:T(8,128)(2,1)} %all-gather.5.cloned.1.call-done.delta_ref, bf16[2,8,192,128]{3,2,1,0:T(8,128)(2,1)} %pad_maximum_fusion.pair_hbm, ...), custom_call_target="tpu_custom_call" | custom-call | flops 1200000000 | bytes 6000000 | tf_op jit(solution)/shard_map/pallas_call | solution.py:330
  164.9 3.6 %all-to-all-done.3 = bf16[16,24,256]{2,1,0:T(8,128)(2,1)} async-done(((bf16[16,24,256]{2,1,0:T(8,128)(2,1)}), bf16[16,24,256]{2,1,0:T(8,128)(2,1)}, u32[]{:S(2)}, u32[]{:S(2)}) %all-to-all-start.3) | async-done | bytes 196640 | tf_op jit(solution)/shard_map/all_to_all | solution.py:329
  168.6 1.9 %shard_map.117 = bf16[128,512]{1,0:T(8,128)(2,1)} custom-call(s32[2,128]{1,0:T(2,128)} %bitcast.26, s32[2,128]{1,0:T(2,128)} %bitcast.28, bf16[384,256]{1,0:T(8,128)(2,1)} %bitcast.12.ret_ref), custom_call_target="tpu_custom_call" | custom-call | flops 50000000 | bytes 400000 | tf_op jit(solution)/shard_map/pallas_call | solution.py:339
Async XLA Ops:
  7.2 80.2 %all-gather.3.cloned.1.call-start = ((), (), s32[]{:S(2)}) async-start(), calls=%async_computation.4 | async-start | bytes 3538944 | tf_op jit(solution)/shard_map/all_gather | solution.py:290
  47.6 111.6 %all-gather.5.cloned.1.call-start = ((), (), s32[]{:S(2)}) async-start(), calls=%async_computation.5 | async-start | bytes 2654208 | tf_op jit(solution)/shard_map/all_gather | solution.py:317
  67.3 11.5 %collective-permute-start = (bf16[8,192,128]{2,1,0:T(8,128)(2,1)}, bf16[8,192,128]{2,1,0:T(8,128)(2,1)S(1)}, u32[]{:S(2)}, u32[]{:S(2)}) collective-permute-start(bf16[8,192,128]{2,1,0:T(8,128)(2,1)} %all_to_all.21), channel_id=1, source_target_pairs={{0,1},{1,0},{2,3},{3,2},{4,5},{5,4},{6,7},{7,6},{8,9},{9,8},{10,11... | collective-permute-start | bytes 1179656 | tf_op jit(solution)/shard_map/ppermute | solution.py:296
  99.5 4.6 %copy-start = (bf16[2,8,192,128]{3,2,1,0:T(8,128)(2,1)S(1)}, bf16[2,8,192,128]{3,2,1,0:T(8,128)(2,1)}, u32[]{:S(2)}) copy-start(bf16[2,8,192,128]{3,2,1,0:T(8,128)(2,1)} %pad_maximum_fusion.pair_hbm) | copy-start | bytes 2359300
  99.5 40.5 %all-to-all-start.2 = ((bf16[8,192,512]{2,1,0:T(8,128)(2,1)}), bf16[8,192,512]{2,1,0:T(8,128)(2,1)}, u32[]{:S(2)}, u32[]{:S(2)}) async-start(bf16[8,192,512]{2,1,0:T(8,128)(2,1)} %shard_map.114), calls=%async_computation.2 | async-start | bytes 3145728 | tf_op jit(solution)/shard_map/all_to_all | solution.py:327
  104.1 32.5 %collective-permute-start.1 = (bf16[2,8,192,128]{3,2,1,0:T(8,128)(2,1)S(1)}, bf16[2,8,192,128]{3,2,1,0:T(8,128)(2,1)}, u32[]{:S(2)}, u32[]{:S(2)}) collective-permute-start(bf16[2,8,192,128]{3,2,1,0:T(8,128)(2,1)S(1)} %copy-done), channel_id=1, source_target_pairs={{0,2},{1,7},{2,4},{3,1},{4,6},{5,3},{6,0},{7,5},{8,10},{9,15},{10,... | collective-permute-start | bytes 2359304 | tf_op jit(solution)/shard_map/ppermute | solution.py:298
  108.6 46.7 %collective-permute-start.3 = (bf16[8,192,128]{2,1,0:T(8,128)(2,1)}, bf16[8,192,128]{2,1,0:T(8,128)(2,1)}, u32[]{:S(2)}, u32[]{:S(2)}) collective-permute-start(bf16[8,192,128]{2,1,0:T(8,128)(2,1)} %all_to_all.21), channel_id=1, source_target_pairs={{0,4},{1,5},{2,6},{3,7},{4,0},{5,1},{6,2},{7,3},{8,12},{9,13},{10,... | collective-permute-start | bytes 1179656 | tf_op jit(solution)/shard_map/ppermute | solution.py:299
  136.5 22.7 %collective-permute-start.2 = (bf16[2,8,192,128]{3,2,1,0:T(8,128)(2,1)}, bf16[2,8,192,128]{3,2,1,0:T(8,128)(2,1)}, u32[]{:S(2)}, u32[]{:S(2)}) collective-permute-start(bf16[2,8,192,128]{3,2,1,0:T(8,128)(2,1)} %collective-permute-done.1.side_hbm), channel_id=1, source_target_pairs={{0,1},{1,0},{2,3},{3,2},{4,5},{5,4},{6,7},{7,6},{8,9},{9,8},{10,11... | collective-permute-start | bytes 2359304 | tf_op jit(solution)/shard_map/ppermute | solution.py:315
  142.5 26.1 %all-to-all-start.3 = ((bf16[16,24,256]{2,1,0:T(8,128)(2,1)}), bf16[16,24,256]{2,1,0:T(8,128)(2,1)}, u32[]{:S(2)}, u32[]{:S(2)}) async-start(bf16[16,24,256]{2,1,0:T(8,128)(2,1)} %shard_map.115), calls=%async_computation.3 | async-start | bytes 393216 | tf_op jit(solution)/shard_map/all_to_all | solution.py:329
  155.3 4.0 %collective-permute-start.4 = (bf16[8,192,128]{2,1,0:T(8,128)(2,1)}, bf16[8,192,128]{2,1,0:T(8,128)(2,1)}, u32[]{:S(2)}, u32[]{:S(2)}) collective-permute-start(bf16[8,192,128]{2,1,0:T(8,128)(2,1)} %collective-permute-done.3.far_hbm), channel_id=1, source_target_pairs={{0,1},{1,0},{2,3},{3,2},{4,5},{5,4},{6,7},{7,6},{8,9},{9,8},{10,11... | collective-permute-start | bytes 1179656 | tf_op jit(solution)/shard_map/ppermute | solution.py:316
Sparse Core Ops, SparseCore 0:
  47.7 39.5 all-gather.2
  93.7 45.0 all-gather.4
where the time goes:
time: 180 us; the launch traced here: 177 us
  blocking collectives  55.3 us (31%)
  starting transfers between devices  40.1 us (22%)
  waiting for transfers between devices  39.1 us (22%)
  Pallas kernels  26.7 us (15%)
  between operations  14.2 us (8%)
  other arithmetic  1.96 us (1%)
    all_to_all x1, blocking collectives, layer(): lax.all_to_all(sent.reshape(16, 24, 512), 'expert', 0, 0, tiled=True)  37.6 us
    ppermute x1, waiting for transfers between devices, layer(): side = lax.ppermute(pair, 'tensor', SIDE)  25.5 us
    all_to_all x1, blocking collectives, layer(): mine = lax.all_to_all(corner, 'dp', 0, 0, tiled=True)  17.7 us
    all_to_all x1, starting transfers between devices, layer(): returned = lax.all_to_all(back, 'expert', 0, 0, tiled=True)  12.8 us
    ppermute x1, starting transfers between devices, layer(): turned = lax.ppermute(mine, 'tensor', SWAP)  9.97 us
    all_gather x1, waiting for transfers between devices, layer(): lax.all_gather(block.reshape(384, 512), 'tensor', axis=0, tiled=True)  6.62 us
    pallas_call x1, Pallas kernels, layer(): call(forward_kernel, shape((192, 768)), [HB, HB, HB, HB], [pltpu.VMEM((8,...  6.16 us
    pallas_call x1, Pallas kernels, layer(): call(slot_kernel, shape((8, 192, 512)), [VM, HB, HB], [pltpu.VMEM((8, 4,...  5.93 us
  transfers between devices with their start and end apart: 9, of which 5 were waited for; matrix products, arithmetic and copies ran while one was open for 1% of the time, Pallas kernels for 9%

commit v1 on v0

--- a/solution.py
+++ b/solution.py
@@ -95,7 +95,12 @@
     return jnp.concatenate([near, rest], axis=0)
 
 
-def forward_kernel(g_hbm, wg_hbm, wu_hbm, wd_hbm, out_ref, buf, wg, wu, wd, sem):
+def slot_term(delta, wg, wu):
+    w = jnp.concatenate([wg.reshape(512, 256), wu.reshape(512, 256)], axis=1)
+    return lax.dot_general(delta, w, LAST, preferred_element_type=F32)
+
+
+def forward_kernel(core_ref, g_hbm, wg_hbm, wu_hbm, wd_hbm, out_ref, term_ref, buf, wg, wu, wd, sem):
     copies = [pltpu.make_async_copy(g_hbm.at[t], buf.at[t], sem.at[0, t]) for t in range(8)]
     down = [
         pltpu.make_async_copy(
@@ -170,30 +175,32 @@
     out_ref[:, 0:256] = (back * up * sig * (1.0 + gate * (1.0 - sig))).astype(BF)
     out_ref[:, 256:512] = (back * act).astype(BF)
     out_ref[:, 512:768] = (act * up).astype(BF)
-
-
-def slot_kernel(delta_ref, wg_hbm, wu_hbm, out_ref, wg, wu, sem):
+    for i in range(4):
+        k = 2 * i + 1 - core_ref[0]
+        term_ref[i] = slot_term(out_ref[:, 0:512], wg[k], wu[k]).astype(BF)
+
+
+def slot_kernel(core_ref, delta_ref, wg_hbm, wu_hbm, add_ref, out_ref, wg, wu, sem):
     copies = [
         [
-            pltpu.make_async_copy(src.at[k], dst.at[k], sem.at[side, k])
+            pltpu.make_async_copy(src.at[2 * i + core_ref[0]], dst.at[i], sem.at[side, i])
             for side, (src, dst) in enumerate(((wg_hbm, wg), (wu_hbm, wu)))
         ]
-        for k in range(8)
+        for i in range(4)
     ]
     for group in copies:
         for copy in group:
             copy.start()
-    for k in range(8):
-        for copy in copies[k]:
+    for i in range(4):
+        for copy in copies[i]:
             copy.wait()
-        w = jnp.concatenate([wg[k].reshape(512, 256), wu[k].reshape(512, 256)], axis=1)
-        term = lax.dot_general(delta_ref[:, 0:512], w, LAST, preferred_element_type=F32)
-        out_ref[k] = term.astype(BF)
+        term = slot_term(delta_ref[:, 0:512], wg[i], wu[i])
+        out_ref[i] = (term + add_ref[i].astype(F32)).astype(BF)
 
 
 def pack_kernel(parts_ref, out_ref):
     total = parts_ref[0].astype(F32)
-    for t in range(1, 8):
+    for t in range(1, 4):
         total = total + parts_ref[t].astype(F32)
     rows = total.astype(BF)
     rest = jnp.zeros((128, 256), F32)
@@ -253,7 +260,7 @@
     ).astype(BF)
 
 
-def call(kernel, out, specs, scratch=(), flops=0, size=0):
+def call(kernel, out, specs, scratch=(), flops=0, size=0, limit=67_043_328):
     single = not isinstance(out, (list, tuple))
     return pl.pallas_call(
         kernel,
@@ -262,7 +269,7 @@
         out_specs=VM if single else [VM] * len(out),
         scratch_shapes=scratch,
         cost_estimate=pl.CostEstimate(flops=flops, bytes_accessed=size, transcendentals=0),
-        compiler_params=pltpu.CompilerParams(vmem_limit_bytes=67_043_328),
+        compiler_params=pltpu.CompilerParams(vmem_limit_bytes=limit),
     )
 
 
@@ -298,10 +305,11 @@
     side = lax.ppermute(pair, "tensor", SIDE)
     far = lax.ppermute(mine, "tensor", FAR)
     whole, pair = lax.optimization_barrier((whole, pair))
-    delta = call(
+    core = lax.bitwise_and(t, 1)
+    delta, terms = call(
         forward_kernel,
-        shape((192, 768)),
-        [HB, HB, HB, HB],
+        [shape((192, 768)), shape((4, 192, 512))],
+        [SM, HB, HB, HB, HB],
         [
             pltpu.VMEM((8, 16, 24, 512), BF),
             pltpu.VMEM((8, 4, 128, 256), BF),
@@ -309,22 +317,25 @@
             pltpu.VMEM((256, 4096), BF),
             dma((4, 8)),
         ],
-        flops=1_300_000_000,
-        size=10_000_000,
-    )(whole.reshape(8, 16, 24, 512), wg, wu, wd)
+        flops=1_700_000_000,
+        size=11_000_000,
+    )(core, whole.reshape(8, 16, 24, 512), wg, wu, wd)
     side2 = lax.ppermute(side, "tensor", SWAP)
     far2 = lax.ppermute(far, "tensor", SWAP)
     deltas = lax.all_gather(delta, "dp", axis=0, tiled=True)
 
+    terms = lax.ppermute(terms, "tensor", SWAP)
     terms = call(
         slot_kernel,
-        shape((8, 192, 512)),
-        [VM, HB, HB],
-        [pltpu.VMEM((8, 4, 128, 256), BF), pltpu.VMEM((8, 4, 128, 256), BF), dma((2, 8))],
-        flops=800_000_000,
-        size=6_000_000,
-    )(delta, wg, wu)
-    parts = lax.all_to_all(terms, "tensor", 0, 0, tiled=True)
+        shape((4, 192, 512)),
+        [SM, VM, HB, HB, VM],
+        [pltpu.VMEM((4, 4, 128, 256), BF), pltpu.VMEM((4, 4, 128, 256), BF), dma((2, 4))],
+        flops=400_000_000,
+        size=4_000_000,
+    )(core, delta, wg, wu, terms)
+    parts = lax.all_to_all(
+        terms, "tensor", 0, 0, axis_index_groups=[[0, 2, 4, 6], [1, 3, 5, 7]], tiled=True
+    )
     back = call(pack_kernel, shape((16, 24, 256)), [VM], flops=10_000_000, size=1_800_000)(parts)
     returned = lax.all_to_all(back, "expert", 0, 0, tiled=True)
     gate_grad, up_grad, down_grad = call(

time: 180 us -> 168 us (0.933)
  the two profiles are of different devices: /device:TPU:1 before, /device:TPU:68 now
where the time goes in v1:
time: 168 us; the launch traced here: 167 us
  blocking collectives  60.8 us (36%)
  starting transfers between devices  32.6 us (19%)
  waiting for transfers between devices  31.6 us (19%)
  Pallas kernels  26.8 us (16%)
  between operations  14.1 us (8%)
    all_to_all x1, blocking collectives, layer(): lax.all_to_all(sent.reshape(16, 24, 512), 'expert', 0, 0, tiled=True)  40.3 us
    all_to_all x1, blocking collectives, layer(): mine = lax.all_to_all(corner, 'dp', 0, 0, tiled=True)  20.4 us
    all_to_all x1, waiting for transfers between devices, layer(): lax.all_to_all(terms, 'tensor', 0, 0, axis_index_groups=[[0, 2, 4, 6], [1...  14.3 us
    all_to_all x1, starting transfers between devices, layer(): returned = lax.all_to_all(back, 'expert', 0, 0, tiled=True)  13.3 us
    pallas_call x1, Pallas kernels, layer(): call(forward_kernel, [shape((192, 768)), shape((4, 192, 512))], [SM, HB,...  7.95 us
    all_to_all x1, waiting for transfers between devices, layer(): returned = lax.all_to_all(back, 'expert', 0, 0, tiled=True)  6.86 us
    all_gather x1, waiting for transfers between devices, layer(): lax.all_gather(block.reshape(384, 512), 'tensor', axis=0, tiled=True)  6.53 us
    pallas_call x1, Pallas kernels, layer(): call(weight_kernel, [shape((512, 256)), shape((512, 256)), shape((256, 51...  5.67 us
  transfers between devices with their start and end apart: 10, of which 5 were waited for; matrix products, arithmetic and copies ran while one was open for 1% of the time, Pallas kernels for 9%

profile of v1, /device:TPU:68, one launch (start us, length us, event | category | flops | bytes accessed | tf_op | source)
XLA Modules:
  0.0 166.9 jit_solution(2477082525762823655)
XLA Ops:
  7.2 0.0 all-gather.3.cloned.1.call-start
  7.2 2.7 %shard_map.111 = bf16[384,512]{1,0:T(8,128)(2,1)} custom-call(s32[1]{0:T(128)} %bitcast.2.t_ref, s32[2,128]{1,0:T(2,128)} %bitcast.26, s32[2,128]{1,0:T(2,128)} %bitcast.28, f32[2,128]{1,0:T(2,128)} %bitcast.30, bf16[128,4096]{1,0:T(8,128)(2,1)} %tok_hbm.1, bf16[128,4096]{1,0:T(8,128)(2,1)} %grad_hbm.1), custom_call_target="tpu_custom_call" | custom-call | flops 100000000 | bytes 700000 | tf_op jit(solution)/shard_map/pallas_call | solution.py:288
  10.0 40.3 %all_to_all.20.block_ref = bf16[16,24,512]{2,1,0:T(8,128)(2,1)} all-to-all(bf16[16,24,512]{2,1,0:T(8,128)(2,1)} %bitcast.24), channel_id=1, replica_groups=mesh['expert'=16,'dp'=8,'tensor'=8] {'expert'}, dimensions={0} | all-to-all | bytes 786432 | tf_op jit(solution)/shard_map/all_to_all | solution.py:296
  50.3 0.0 all-gather.3.cloned.1.call-update
  50.3 0.0 all-gather.5.cloned.1.call-start
  50.4 1.9 %shard_map.112 = bf16[8,192,128]{2,1,0:T(8,128)(2,1)} custom-call(bf16[16,24,512]{2,1,0:T(8,128)(2,1)} %all_to_all.20.block_ref), custom_call_target="tpu_custom_call" | custom-call | flops 20000000 | bytes 800000 | tf_op jit(solution)/shard_map/pallas_call | solution.py:299
  52.3 20.4 %all_to_all.21 = bf16[8,192,128]{2,1,0:T(8,128)(2,1)S(1)} all-to-all(bf16[8,192,128]{2,1,0:T(8,128)(2,1)} %shard_map.112), channel_id=1, replica_groups=mesh['expert'=16,'dp'=8,'tensor'=8] {'dp'}, dimensions={0} | all-to-all | bytes 786432 | tf_op jit(solution)/shard_map/all_to_all | solution.py:302
  72.8 0.0 copy-start
  72.8 1.9 %collective-permute-start = (bf16[8,192,128]{2,1,0:T(8,128)(2,1)S(1)}, bf16[8,192,128]{2,1,0:T(8,128)(2,1)S(1)}, u32[]{:S(2)}, u32[]{:S(2)}) collective-permute-start(bf16[8,192,128]{2,1,0:T(8,128)(2,1)S(1)} %all_to_all.21), channel_id=1, source_target_pairs={{0,1},{1,0},{2,3},{3,2},{4,5},{5,4},{6,7},{7,6},{8,9},{9,8},{10,11... | collective-permute-start | bytes 1179656 | tf_op jit(solution)/shard_map/ppermute | solution.py:303
  74.7 1.8 %collective-permute-done = bf16[8,192,128]{2,1,0:T(8,128)(2,1)S(1)} collective-permute-done((bf16[8,192,128]{2,1,0:T(8,128)(2,1)S(1)}, bf16[8,192,128]{2,1,0:T(8,128)(2,1)S(1)}, u32[]{:S(2)}, u32[]{:S(2)}) %collective-permute-start) | collective-permute-done | bytes 393248 | tf_op jit(solution)/shard_map/ppermute | solution.py:303
  76.5 0.0 copy-done
  76.5 1.0 pad_maximum_fusion.pair_hbm
  77.5 6.5 %all-gather.3.cloned.1.call-done = bf16[3072,512]{1,0:T(8,128)(2,1)} async-done(((bf16[384,512]{1,0:T(8,128)(2,1)}), bf16[3072,512]{1,0:T(8,128)(2,1)}) %all-gather.3.cloned.1.call-update) | async-done | bytes 3145744 | tf_op jit(solution)/shard_map/all_gather | solution.py:297
  84.0 7.9 %shard_map.113 = (bf16[192,768]{1,0:T(8,128)(2,1)}, bf16[4,192,512]{2,1,0:T(8,128)(2,1)}) custom-call(s32[1]{0:T(128)S(6)} %and.4.core_ref, bf16[8,16,24,512]{3,2,1,0:T(8,128)(2,1)} %bitcast.21, bf16[8,4,128,256]{3,2,1,0:T(8,128)(2,1)} %bitcast.16, bf16[8,4,128,256]{3,2,1,0:T(8,128)(2,1)} %bitcast.18, bf16[256,4096]{1,0:T(8,128)(2,1)} %bitcast.22), custom_call_target="tpu_custom_call" | custom-call | flops 1700000000 | bytes 11000000 | tf_op jit(solution)/shard_map/pallas_call | solution.py:309
  91.9 0.0 all-gather.5.cloned.1.call-update
  92.0 2.1 %collective-permute-start.1 = (bf16[4,192,512]{2,1,0:T(8,128)(2,1)}, bf16[4,192,512]{2,1,0:T(8,128)(2,1)}, u32[]{:S(2)}, u32[]{:S(2)}) collective-permute-start(bf16[4,192,512]{2,1,0:T(8,128)(2,1)} %get-tuple-element.15), channel_id=1, source_target_pairs={{0,1},{1,0},{2,3},{3,2},{4,5},{5,4},{6,7},{7,6},{8,9},{9,8},{10,11... | collective-permute-start | bytes 2359304 | tf_op jit(solution)/shard_map/ppermute | solution.py:327
  94.1 3.4 %collective-permute-start.2 = (bf16[2,8,192,128]{3,2,1,0:T(8,128)(2,1)}, bf16[2,8,192,128]{3,2,1,0:T(8,128)(2,1)}, u32[]{:S(2)}, u32[]{:S(2)}) collective-permute-start(bf16[2,8,192,128]{3,2,1,0:T(8,128)(2,1)} %pad_maximum_fusion.pair_hbm), channel_id=1, source_target_pairs={{0,2},{1,7},{2,4},{3,1},{4,6},{5,3},{6,0},{7,5},{8,10},{9,15},{10,... | collective-permute-start | bytes 2359304 | tf_op jit(solution)/shard_map/ppermute | solution.py:305
  97.6 0.0 collective-permute-done.1.add_ref
  97.6 4.5 %shard_map.114 = bf16[4,192,512]{2,1,0:T(8,128)(2,1)} custom-call(s32[1]{0:T(128)S(6)} %and.4.core_ref, bf16[192,768]{1,0:T(8,128)(2,1)} %get-tuple-element.14.delta_ref, bf16[8,4,128,256]{3,2,1,0:T(8,128)(2,1)} %bitcast.17, bf16[8,4,128,256]{3,2,1,0:T(8,128)(2,1)} %bitcast.19, bf16[4,192,512]{2,1,0:T(8,128)(2,1)} %collective-permute-done.1.add_ref), custom_call_target="tpu_custom_call" | custom-call | flops 400000000 | bytes 4000000 | tf_op jit(solution)/shard_map/pallas_call | solution.py:328
  102.1 5.1 %all-to-all-start.2 = ((bf16[4,192,512]{2,1,0:T(8,128)(2,1)}), bf16[4,192,512]{2,1,0:T(8,128)(2,1)}, u32[]{:S(2)}, u32[]{:S(2)}) async-start(bf16[4,192,512]{2,1,0:T(8,128)(2,1)} %shard_map.114), calls=%async_computation.2 | async-start | bytes 1572864 | tf_op jit(solution)/shard_map/all_to_all | solution.py:336
  107.2 2.0 %collective-permute-start.4 = (bf16[8,192,128]{2,1,0:T(8,128)(2,1)}, bf16[8,192,128]{2,1,0:T(8,128)(2,1)}, u32[]{:S(2)}, u32[]{:S(2)}) collective-permute-start(bf16[8,192,128]{2,1,0:T(8,128)(2,1)} %copy-done), channel_id=1, source_target_pairs={{0,4},{1,5},{2,6},{3,7},{4,0},{5,1},{6,2},{7,3},{8,12},{9,13},{10,... | collective-permute-start | bytes 1179656 | tf_op jit(solution)/shard_map/ppermute | solution.py:306
  109.2 0.0 collective-permute-done.2.side_hbm
  109.2 2.8 %collective-permute-start.3 = (bf16[2,8,192,128]{3,2,1,0:T(8,128)(2,1)}, bf16[2,8,192,128]{3,2,1,0:T(8,128)(2,1)}, u32[]{:S(2)}, u32[]{:S(2)}) collective-permute-start(bf16[2,8,192,128]{3,2,1,0:T(8,128)(2,1)} %collective-permute-done.2.side_hbm), channel_id=1, source_target_pairs={{0,1},{1,0},{2,3},{3,2},{4,5},{5,4},{6,7},{7,6},{8,9},{9,8},{10,11... | collective-permute-start | bytes 2359304 | tf_op jit(solution)/shard_map/ppermute | solution.py:323
  112.0 14.3 %all-to-all-done.2.parts_ref = bf16[4,192,512]{2,1,0:T(8,128)(2,1)} async-done(((bf16[4,192,512]{2,1,0:T(8,128)(2,1)}), bf16[4,192,512]{2,1,0:T(8,128)(2,1)}, u32[]{:S(2)}, u32[]{:S(2)}) %all-to-all-start.2) | async-done | bytes 786464 | tf_op jit(solution)/shard_map/all_to_all | solution.py:336
  126.3 2.1 %shard_map.115 = bf16[16,24,256]{2,1,0:T(8,128)(2,1)} custom-call(bf16[4,192,512]{2,1,0:T(8,128)(2,1)} %all-to-all-done.2.parts_ref), custom_call_target="tpu_custom_call" | custom-call | flops 10000000 | bytes 1800000 | tf_op jit(solution)/shard_map/pallas_call | solution.py:339
  128.3 13.3 %all-to-all-start.3 = ((bf16[16,24,256]{2,1,0:T(8,128)(2,1)}), bf16[16,24,256]{2,1,0:T(8,128)(2,1)}, u32[]{:S(2)}, u32[]{:S(2)}) async-start(bf16[16,24,256]{2,1,0:T(8,128)(2,1)} %shard_map.115), calls=%async_computation.3 | async-start | bytes 393216 | tf_op jit(solution)/shard_map/all_to_all | solution.py:340
  141.7 0.0 collective-permute-done.4.far_hbm
  141.7 1.9 %collective-permute-start.5 = (bf16[8,192,128]{2,1,0:T(8,128)(2,1)}, bf16[8,192,128]{2,1,0:T(8,128)(2,1)}, u32[]{:S(2)}, u32[]{:S(2)}) collective-permute-start(bf16[8,192,128]{2,1,0:T(8,128)(2,1)} %collective-permute-done.4.far_hbm), channel_id=1, source_target_pairs={{0,1},{1,0},{2,3},{3,2},{4,5},{5,4},{6,7},{7,6},{8,9},{9,8},{10,11... | collective-permute-start | bytes 1179656 | tf_op jit(solution)/shard_map/ppermute | solution.py:324
  143.6 2.0 %collective-permute-done.5.far2_hbm = bf16[8,192,128]{2,1,0:T(8,128)(2,1)} collective-permute-done((bf16[8,192,128]{2,1,0:T(8,128)(2,1)}, bf16[8,192,128]{2,1,0:T(8,128)(2,1)}, u32[]{:S(2)}, u32[]{:S(2)}) %collective-permute-start.5) | collective-permute-done | bytes 393248 | tf_op jit(solution)/shard_map/ppermute | solution.py:324
  145.6 0.0 collective-permute-done.3.side2_hbm
  145.6 0.0 all-gather.5.cloned.1.call-done.delta_ref
  145.6 5.7 %shard_map.116 = (bf16[512,256]{1,0:T(8,128)(2,1)}, bf16[512,256]{1,0:T(8,128)(2,1)}, bf16[256,512]{1,0:T(8,128)(2,1)}) custom-call(s32[1]{0:T(128)} %bitcast.2.t_ref, bf16[1536,768]{1,0:T(8,128)(2,1)} %all-gather.5.cloned.1.call-done.delta_ref, bf16[2,8,192,128]{3,2,1,0:T(8,128)(2,1)} %pad_maximum_fusion.pair_hbm, ...), custom_call_target="tpu_custom_call" | custom-call | flops 1200000000 | bytes 6000000 | tf_op jit(solution)/shard_map/pallas_call | solution.py:341
  151.3 6.9 %all-to-all-done.3 = bf16[16,24,256]{2,1,0:T(8,128)(2,1)} async-done(((bf16[16,24,256]{2,1,0:T(8,128)(2,1)}), bf16[16,24,256]{2,1,0:T(8,128)(2,1)}, u32[]{:S(2)}, u32[]{:S(2)}) %all-to-all-start.3) | async-done | bytes 196640 | tf_op jit(solution)/shard_map/all_to_all | solution.py:340
  158.2 1.9 %shard_map.117 = bf16[128,512]{1,0:T(8,128)(2,1)} custom-call(s32[2,128]{1,0:T(2,128)} %bitcast.27, s32[2,128]{1,0:T(2,128)} %bitcast.29, bf16[384,256]{1,0:T(8,128)(2,1)} %bitcast.12.ret_ref), custom_call_target="tpu_custom_call" | custom-call | flops 50000000 | bytes 400000 | tf_op jit(solution)/shard_map/pallas_call | solution.py:350
Async XLA Ops:
  7.2 76.8 %all-gather.3.cloned.1.call-start = ((), (), s32[]{:S(2)}) async-start(), calls=%async_computation.4 | async-start | bytes 3538944 | tf_op jit(solution)/shard_map/all_gather | solution.py:297
  50.3 95.3 %all-gather.5.cloned.1.call-start = ((), (), s32[]{:S(2)}) async-start(), calls=%async_computation.5 | async-start | bytes 2654208 | tf_op jit(solution)/shard_map/all_gather | solution.py:325
  72.8 3.8 %copy-start = (bf16[8,192,128]{2,1,0:T(8,128)(2,1)}, bf16[8,192,128]{2,1,0:T(8,128)(2,1)S(1)}, u32[]{:S(2)}) copy-start(bf16[8,192,128]{2,1,0:T(8,128)(2,1)S(1)} %all_to_all.21) | copy-start | bytes 1179652
  72.8 3.7 %collective-permute-start = (bf16[8,192,128]{2,1,0:T(8,128)(2,1)S(1)}, bf16[8,192,128]{2,1,0:T(8,128)(2,1)S(1)}, u32[]{:S(2)}, u32[]{:S(2)}) collective-permute-start(bf16[8,192,128]{2,1,0:T(8,128)(2,1)S(1)} %all_to_all.21), channel_id=1, source_target_pairs={{0,1},{1,0},{2,3},{3,2},{4,5},{5,4},{6,7},{7,6},{8,9},{9,8},{10,11... | collective-permute-start | bytes 1179656 | tf_op jit(solution)/shard_map/ppermute | solution.py:303
  92.0 5.6 %collective-permute-start.1 = (bf16[4,192,512]{2,1,0:T(8,128)(2,1)}, bf16[4,192,512]{2,1,0:T(8,128)(2,1)}, u32[]{:S(2)}, u32[]{:S(2)}) collective-permute-start(bf16[4,192,512]{2,1,0:T(8,128)(2,1)} %get-tuple-element.15), channel_id=1, source_target_pairs={{0,1},{1,0},{2,3},{3,2},{4,5},{5,4},{6,7},{7,6},{8,9},{9,8},{10,11... | collective-permute-start | bytes 2359304 | tf_op jit(solution)/shard_map/ppermute | solution.py:327
  94.1 15.0 %collective-permute-start.2 = (bf16[2,8,192,128]{3,2,1,0:T(8,128)(2,1)}, bf16[2,8,192,128]{3,2,1,0:T(8,128)(2,1)}, u32[]{:S(2)}, u32[]{:S(2)}) collective-permute-start(bf16[2,8,192,128]{3,2,1,0:T(8,128)(2,1)} %pad_maximum_fusion.pair_hbm), channel_id=1, source_target_pairs={{0,2},{1,7},{2,4},{3,1},{4,6},{5,3},{6,0},{7,5},{8,10},{9,15},{10,... | collective-permute-start | bytes 2359304 | tf_op jit(solution)/shard_map/ppermute | solution.py:305
  102.1 24.1 %all-to-all-start.2 = ((bf16[4,192,512]{2,1,0:T(8,128)(2,1)}), bf16[4,192,512]{2,1,0:T(8,128)(2,1)}, u32[]{:S(2)}, u32[]{:S(2)}) async-start(bf16[4,192,512]{2,1,0:T(8,128)(2,1)} %shard_map.114), calls=%async_computation.2 | async-start | bytes 1572864 | tf_op jit(solution)/shard_map/all_to_all | solution.py:336
  107.2 34.5 %collective-permute-start.4 = (bf16[8,192,128]{2,1,0:T(8,128)(2,1)}, bf16[8,192,128]{2,1,0:T(8,128)(2,1)}, u32[]{:S(2)}, u32[]{:S(2)}) collective-permute-start(bf16[8,192,128]{2,1,0:T(8,128)(2,1)} %copy-done), channel_id=1, source_target_pairs={{0,4},{1,5},{2,6},{3,7},{4,0},{5,1},{6,2},{7,3},{8,12},{9,13},{10,... | collective-permute-start | bytes 1179656 | tf_op jit(solution)/shard_map/ppermute | solution.py:306
  109.2 36.4 %collective-permute-start.3 = (bf16[2,8,192,128]{3,2,1,0:T(8,128)(2,1)}, bf16[2,8,192,128]{3,2,1,0:T(8,128)(2,1)}, u32[]{:S(2)}, u32[]{:S(2)}) collective-permute-start(bf16[2,8,192,128]{3,2,1,0:T(8,128)(2,1)} %collective-permute-done.2.side_hbm), channel_id=1, source_target_pairs={{0,1},{1,0},{2,3},{3,2},{4,5},{5,4},{6,7},{7,6},{8,9},{9,8},{10,11... | collective-permute-start | bytes 2359304 | tf_op jit(solution)/shard_map/ppermute | solution.py:323
  128.3 29.8 %all-to-all-start.3 = ((bf16[16,24,256]{2,1,0:T(8,128)(2,1)}), bf16[16,24,256]{2,1,0:T(8,128)(2,1)}, u32[]{:S(2)}, u32[]{:S(2)}) async-start(bf16[16,24,256]{2,1,0:T(8,128)(2,1)} %shard_map.115), calls=%async_computation.3 | async-start | bytes 393216 | tf_op jit(solution)/shard_map/all_to_all | solution.py:340
  141.7 4.0 %collective-permute-start.5 = (bf16[8,192,128]{2,1,0:T(8,128)(2,1)}, bf16[8,192,128]{2,1,0:T(8,128)(2,1)}, u32[]{:S(2)}, u32[]{:S(2)}) collective-permute-start(bf16[8,192,128]{2,1,0:T(8,128)(2,1)} %collective-permute-done.4.far_hbm), channel_id=1, source_target_pairs={{0,1},{1,0},{2,3},{3,2},{4,5},{5,4},{6,7},{7,6},{8,9},{9,8},{10,11... | collective-permute-start | bytes 1179656 | tf_op jit(solution)/shard_map/ppermute | solution.py:324
Sparse Core Ops, SparseCore 0:
  50.4 33.4 all-gather.2
  92.1 50.3 all-gather.4

commit v2 on v1

--- a/solution.py
+++ b/solution.py
@@ -95,96 +95,109 @@
     return jnp.concatenate([near, rest], axis=0)
 
 
-def slot_term(delta, wg, wu):
-    w = jnp.concatenate([wg.reshape(512, 256), wu.reshape(512, 256)], axis=1)
-    return lax.dot_general(delta, w, LAST, preferred_element_type=F32)
-
-
-def forward_kernel(core_ref, g_hbm, wg_hbm, wu_hbm, wd_hbm, out_ref, term_ref, buf, wg, wu, wd, sem):
-    copies = [pltpu.make_async_copy(g_hbm.at[t], buf.at[t], sem.at[0, t]) for t in range(8)]
-    down = [
-        pltpu.make_async_copy(
-            wd_hbm.at[:, pl.ds(q * 2048, 2048)], wd.at[:, pl.ds(q * 2048, 2048)], sem.at[1, q]
-        )
-        for q in range(2)
-    ]
-    first = [
-        [
-            pltpu.make_async_copy(
-                src.at[pl.ds(q * 4, 4)], dst.at[pl.ds(q * 4, 4)], sem.at[2 + side, q]
-            )
-            for side, (src, dst) in enumerate(((wg_hbm, wg), (wu_hbm, wu)))
-        ]
-        for q in range(2)
-    ]
-    for copy in copies[4:8] + down + copies[0:4] + first[0] + first[1]:
+def forward_kernel(core_ref, g_hbm, wg_hbm, wu_hbm, wd_hbm, out_ref, term_ref, x, w, wd, sem):
+    def load_rows(kind):
+        copies = []
+        for unit in range(4):
+            t = kind * 4 + unit
+            lanes = pl.ds(unit * 512, 512)
+            for q in range(2):
+                for part, row in enumerate((q * 8, 16)):
+                    copies.append(
+                        pltpu.make_async_copy(
+                            g_hbm.at[t, :, pl.ds(row, 8), :],
+                            x.at[kind, q, part, :, :, lanes],
+                            sem.at[kind, unit * 4 + q * 2 + part],
+                        )
+                    )
+        return copies
+
+    def load_down(q):
+        copies = []
+        for j in range(4):
+            for unit in range(4):
+                copies.append(
+                    pltpu.make_async_copy(
+                        wd_hbm.at[:, pl.ds((q * 4 + j) * 512 + unit * 128, 128)],
+                        wd.at[q, :, pl.ds(unit * 512 + j * 128, 128)],
+                        sem.at[2 + q, unit * 4 + j],
+                    )
+                )
+        return copies
+
+    def load_first(q):
+        copies = []
+        for unit in range(4):
+            for side, src in enumerate((wg_hbm, wu_hbm)):
+                copies.append(
+                    pltpu.make_async_copy(
+                        src.at[pl.ds(q * 4, 4), unit],
+                        w.at[q, unit, :, :, pl.ds(side * 256, 256)],
+                        sem.at[4 + q, unit * 2 + side],
+                    )
+                )
+        return copies
+
+    grads, toks = load_rows(1), load_rows(0)
+    down = [load_down(q) for q in range(2)]
+    first = [load_first(q) for q in range(2)]
+    for copy in grads + down[0] + down[1] + toks + first[0] + first[1]:
         copy.start()
-
-    def rows(units, q):
-        return jnp.concatenate(
-            [
-                jnp.concatenate(
-                    [
-                        buf[t, :, q * 8 : (q + 1) * 8, :].reshape(128, 512),
-                        buf[t, :, 16:24, :].reshape(128, 512),
-                    ],
-                    axis=0,
-                )
-                for t in units
-            ],
-            axis=1,
-        )
-
-    for copy in copies[4:8]:
+    for copy in grads:
         copy.wait()
     terms = []
     for q in range(2):
-        down[q].wait()
-        w = jnp.concatenate(
-            [
-                wd[:, (q * 4 + j) * 512 + unit * 128 : (q * 4 + j) * 512 + (unit + 1) * 128]
-                for unit in range(4)
-                for j in range(4)
-            ],
-            axis=1,
-        )
+        for copy in down[q]:
+            copy.wait()
         terms.append(
-            lax.dot_general(rows(range(4, 8), q), w, LAST, preferred_element_type=F32)
+            lax.dot_general(
+                x[1, q].reshape(256, 2048), wd[q], LAST, preferred_element_type=F32
+            )
         )
     back = settle(*terms)
-    for copy in copies[0:4]:
+    for copy in toks:
         copy.wait()
     terms = []
     for q in range(2):
         for copy in first[q]:
             copy.wait()
-        w = jnp.concatenate(
-            [
-                jnp.concatenate(
-                    [m[q * 4 : (q + 1) * 4, unit].reshape(512, 256) for unit in range(4)], axis=0
-                )
-                for m in (wg, wu)
-            ],
-            axis=1,
+        terms.append(
+            jnp.dot(
+                x[0, q].reshape(256, 2048),
+                w[q].reshape(2048, 512),
+                preferred_element_type=F32,
+            )
         )
-        terms.append(jnp.dot(rows(range(4), q), w, preferred_element_type=F32))
     both = settle(*terms)
     gate, up = both[:, 0:256], both[:, 256:512]
     sig = jax.nn.sigmoid(gate)
     act = gate * sig
-    out_ref[:, 0:256] = (back * up * sig * (1.0 + gate * (1.0 - sig))).astype(BF)
-    out_ref[:, 256:512] = (back * act).astype(BF)
+    deltas = jnp.concatenate(
+        [
+            (back * up * sig * (1.0 + gate * (1.0 - sig))).astype(BF),
+            (back * act).astype(BF),
+        ],
+        axis=1,
+    )
+    out_ref[:, 0:512] = deltas
     out_ref[:, 512:768] = (act * up).astype(BF)
     for i in range(4):
         k = 2 * i + 1 - core_ref[0]
-        term_ref[i] = slot_term(out_ref[:, 0:512], wg[k], wu[k]).astype(BF)
-
-
-def slot_kernel(core_ref, delta_ref, wg_hbm, wu_hbm, add_ref, out_ref, wg, wu, sem):
+        block = w[i // 2, :, lax.rem(k, 4)].reshape(512, 512)
+        term_ref[i] = lax.dot_general(
+            deltas, block, LAST, preferred_element_type=F32
+        ).astype(BF)
+
+
+def slot_kernel(core_ref, delta_ref, wg_hbm, wu_hbm, out_ref, w, sem):
     copies = [
         [
-            pltpu.make_async_copy(src.at[2 * i + core_ref[0]], dst.at[i], sem.at[side, i])
-            for side, (src, dst) in enumerate(((wg_hbm, wg), (wu_hbm, wu)))
+            pltpu.make_async_copy(
+                src.at[2 * i + core_ref[0]],
+                w.at[i, :, :, pl.ds(side * 256, 256)],
+                sem.at[side, i],
+            )
+            for side, src in enumerate((wg_hbm, wu_hbm))
         ]
         for i in range(4)
     ]
@@ -194,8 +207,9 @@
     for i in range(4):
         for copy in copies[i]:
             copy.wait()
-        term = slot_term(delta_ref[:, 0:512], wg[i], wu[i])
-        out_ref[i] = (term + add_ref[i].astype(F32)).astype(BF)
+        out_ref[i] = lax.dot_general(
+            delta_ref[:, 0:512], w[i].reshape(512, 512), LAST, preferred_element_type=F32
+        ).astype(BF)
 
 
 def pack_kernel(parts_ref, out_ref):
@@ -311,11 +325,10 @@
         [shape((192, 768)), shape((4, 192, 512))],
         [SM, HB, HB, HB, HB],
         [
-            pltpu.VMEM((8, 16, 24, 512), BF),
-            pltpu.VMEM((8, 4, 128, 256), BF),
-            pltpu.VMEM((8, 4, 128, 256), BF),
-            pltpu.VMEM((256, 4096), BF),
-            dma((4, 8)),
+            pltpu.VMEM((2, 2, 2, 16, 8, 2048), BF),
+            pltpu.VMEM((2, 4, 4, 128, 512), BF),
+            pltpu.VMEM((2, 256, 2048), BF),
+            dma((6, 16)),
         ],
         flops=1_700_000_000,
         size=11_000_000,
@@ -324,15 +337,16 @@
     far2 = lax.ppermute(far, "tensor", SWAP)
     deltas = lax.all_gather(delta, "dp", axis=0, tiled=True)
 
-    terms = lax.ppermute(terms, "tensor", SWAP)
+    others = lax.ppermute(terms, "tensor", SWAP)
     terms = call(
         slot_kernel,
         shape((4, 192, 512)),
-        [SM, VM, HB, HB, VM],
-        [pltpu.VMEM((4, 4, 128, 256), BF), pltpu.VMEM((4, 4, 128, 256), BF), dma((2, 4))],
+        [SM, VM, HB, HB],
+        [pltpu.VMEM((4, 4, 128, 512), BF), dma((2, 4))],
         flops=400_000_000,
         size=4_000_000,
-    )(core, delta, wg, wu, terms)
+    )(core, delta, wg, wu)
+    terms = (terms.astype(F32) + others.astype(F32)).astype(BF)
     parts = lax.all_to_all(
         terms, "tensor", 0, 0, axis_index_groups=[[0, 2, 4, 6], [1, 3, 5, 7]], tiled=True
     )

time: 168 us -> 171 us (1.018)
  other arithmetic: 0.96 us -> 4.44 us
    convert_element_type x0 -> x1, other arithmetic: none -> 2.47 us  [layer(): terms = (terms.astype(F32) + others.astype(F32)).astype(BF)]
  transfers between devices with their start and end apart: 10 -> 10, of which waited for: 5 -> 5; matrix products, arithmetic and copies ran while one was open for 1% -> 3% of each run, Pallas kernels for 9% -> 8%
where the time goes in v2:
time: 171 us; the launch traced here: 170 us
  blocking collectives  60.9 us (36%)
  starting transfers between devices  32.6 us (19%)
  waiting for transfers between devices  30.5 us (18%)
  Pallas kernels  27.5 us (16%)
  between operations  14.1 us (8%)
  other arithmetic  4.44 us (3%)
    all_to_all x1, blocking collectives, layer(): lax.all_to_all(sent.reshape(16, 24, 512), 'expert', 0, 0, tiled=True)  40.3 us
    all_to_all x1, blocking collectives, layer(): mine = lax.all_to_all(corner, 'dp', 0, 0, tiled=True)  20.5 us
    all_to_all x1, waiting for transfers between devices, layer(): lax.all_to_all(terms, 'tensor', 0, 0, axis_index_groups=[[0, 2, 4, 6], [1...  14.3 us
    all_to_all x1, starting transfers between devices, layer(): returned = lax.all_to_all(back, 'expert', 0, 0, tiled=True)  13.3 us
    pallas_call x1, Pallas kernels, layer(): call(forward_kernel, [shape((192, 768)), shape((4, 192, 512))], [SM, HB,...  8.93 us
    all_to_all x1, waiting for transfers between devices, layer(): returned = lax.all_to_all(back, 'expert', 0, 0, tiled=True)  6.87 us
    pallas_call x1, Pallas kernels, layer(): call(weight_kernel, [shape((512, 256)), shape((512, 256)), shape((256, 51...  5.67 us
    all_gather x1, waiting for transfers between devices, layer(): lax.all_gather(block.reshape(384, 512), 'tensor', axis=0, tiled=True)  5.35 us
  transfers between devices with their start and end apart: 10, of which 5 were waited for; matrix products, arithmetic and copies ran while one was open for 3% of the time, Pallas kernels for 8%

profile of v2, /device:TPU:68, one launch (start us, length us, event | category | flops | bytes accessed | tf_op | source)
XLA Modules:
  0.0 170.1 jit_solution(2159616533061673998)
XLA Ops:
  7.2 0.0 all-gather.3.cloned.1.call-start
  7.2 2.7 %shard_map.111 = bf16[384,512]{1,0:T(8,128)(2,1)} custom-call(s32[1]{0:T(128)} %bitcast.2.t_ref, s32[2,128]{1,0:T(2,128)} %bitcast.25, s32[2,128]{1,0:T(2,128)} %bitcast.27, f32[2,128]{1,0:T(2,128)} %bitcast.29, bf16[128,4096]{1,0:T(8,128)(2,1)} %tok_hbm.1, bf16[128,4096]{1,0:T(8,128)(2,1)} %grad_hbm.1), custom_call_target="tpu_custom_call" | custom-call | flops 100000000 | bytes 700000 | tf_op jit(solution)/shard_map/pallas_call | solution.py:302
  10.0 40.3 %all_to_all.20.block_ref = bf16[16,24,512]{2,1,0:T(8,128)(2,1)} all-to-all(bf16[16,24,512]{2,1,0:T(8,128)(2,1)} %bitcast.23), channel_id=1, replica_groups=mesh['expert'=16,'dp'=8,'tensor'=8] {'expert'}, dimensions={0} | all-to-all | bytes 786432 | tf_op jit(solution)/shard_map/all_to_all | solution.py:310
  50.3 0.0 all-gather.3.cloned.1.call-update
  50.3 0.0 all-gather.5.cloned.1.call-start
  50.4 1.9 %shard_map.112 = bf16[8,192,128]{2,1,0:T(8,128)(2,1)} custom-call(bf16[16,24,512]{2,1,0:T(8,128)(2,1)} %all_to_all.20.block_ref), custom_call_target="tpu_custom_call" | custom-call | flops 20000000 | bytes 800000 | tf_op jit(solution)/shard_map/pallas_call | solution.py:313
  52.3 20.5 %all_to_all.21 = bf16[8,192,128]{2,1,0:T(8,128)(2,1)} all-to-all(bf16[8,192,128]{2,1,0:T(8,128)(2,1)} %shard_map.112), channel_id=1, replica_groups=mesh['expert'=16,'dp'=8,'tensor'=8] {'dp'}, dimensions={0} | all-to-all | bytes 786432 | tf_op jit(solution)/shard_map/all_to_all | solution.py:316
  72.8 1.9 %collective-permute-start = (bf16[8,192,128]{2,1,0:T(8,128)(2,1)}, bf16[8,192,128]{2,1,0:T(8,128)(2,1)S(1)}, u32[]{:S(2)}, u32[]{:S(2)}) collective-permute-start(bf16[8,192,128]{2,1,0:T(8,128)(2,1)} %all_to_all.21), channel_id=1, source_target_pairs={{0,1},{1,0},{2,3},{3,2},{4,5},{5,4},{6,7},{7,6},{8,9},{9,8},{10,11... | collective-permute-start | bytes 1179656 | tf_op jit(solution)/shard_map/ppermute | solution.py:317
  74.8 1.9 %collective-permute-done = bf16[8,192,128]{2,1,0:T(8,128)(2,1)S(1)} collective-permute-done((bf16[8,192,128]{2,1,0:T(8,128)(2,1)}, bf16[8,192,128]{2,1,0:T(8,128)(2,1)S(1)}, u32[]{:S(2)}, u32[]{:S(2)}) %collective-permute-start) | collective-permute-done | bytes 393248 | tf_op jit(solution)/shard_map/ppermute | solution.py:317
  76.7 2.0 %pad_maximum_fusion.pair_hbm = bf16[2,8,192,128]{3,2,1,0:T(8,128)(2,1)} fusion(bf16[1,8,192,128]{3,2,1,0:T(8,128)(2,1)S(1)} %bitcast.24, bf16[1,8,192,128]{3,2,1,0:T(8,128)(2,1)} %bitcast.6), kind=kLoop, calls=%fused_computation.1 | loop fusion | flops 393216 | bytes 1572864 | tf_op jit(solution)/shard_map/concatenate | solution.py:318
  78.6 5.4 %all-gather.3.cloned.1.call-done = bf16[3072,512]{1,0:T(8,128)(2,1)} async-done(((bf16[384,512]{1,0:T(8,128)(2,1)}), bf16[3072,512]{1,0:T(8,128)(2,1)}) %all-gather.3.cloned.1.call-update) | async-done | bytes 3145744 | tf_op jit(solution)/shard_map/all_gather | solution.py:311
  84.0 8.9 %shard_map.113 = (bf16[192,768]{1,0:T(8,128)(2,1)}, bf16[4,192,512]{2,1,0:T(8,128)(2,1)}) custom-call(s32[1]{0:T(128)S(6)} %and.4.core_ref, bf16[8,16,24,512]{3,2,1,0:T(8,128)(2,1)} %bitcast.21, bf16[8,4,128,256]{3,2,1,0:T(8,128)(2,1)} %bitcast.16, bf16[8,4,128,256]{3,2,1,0:T(8,128)(2,1)} %bitcast.18, bf16[256,4096]{1,0:T(8,128)(2,1)} %bitcast.22), custom_call_target="tpu_custom_call" | custom-call | flops 1700000000 | bytes 11000000 | tf_op jit(solution)/shard_map/pallas_call | solution.py:323
  92.9 0.0 all-gather.5.cloned.1.call-update
  93.0 2.1 %collective-permute-start.1 = (bf16[4,192,512]{2,1,0:T(8,128)(2,1)}, bf16[4,192,512]{2,1,0:T(8,128)(2,1)}, u32[]{:S(2)}, u32[]{:S(2)}) collective-permute-start(bf16[4,192,512]{2,1,0:T(8,128)(2,1)} %get-tuple-element.15), channel_id=1, source_target_pairs={{0,1},{1,0},{2,3},{3,2},{4,5},{5,4},{6,7},{7,6},{8,9},{9,8},{10,11... | collective-permute-start | bytes 2359304 | tf_op jit(solution)/shard_map/ppermute | solution.py:340
  95.1 3.4 %collective-permute-start.2 = (bf16[2,8,192,128]{3,2,1,0:T(8,128)(2,1)}, bf16[2,8,192,128]{3,2,1,0:T(8,128)(2,1)}, u32[]{:S(2)}, u32[]{:S(2)}) collective-permute-start(bf16[2,8,192,128]{3,2,1,0:T(8,128)(2,1)} %pad_maximum_fusion.pair_hbm), channel_id=1, source_target_pairs={{0,2},{1,7},{2,4},{3,1},{4,6},{5,3},{6,0},{7,5},{8,10},{9,15},{10,... | collective-permute-start | bytes 2359304 | tf_op jit(solution)/shard_map/ppermute | solution.py:319
  98.5 4.3 %shard_map.114 = bf16[4,192,512]{2,1,0:T(8,128)(2,1)} custom-call(s32[1]{0:T(128)S(6)} %and.4.core_ref, bf16[192,768]{1,0:T(8,128)(2,1)} %get-tuple-element.14.delta_ref, bf16[8,4,128,256]{3,2,1,0:T(8,128)(2,1)} %bitcast.17, bf16[8,4,128,256]{3,2,1,0:T(8,128)(2,1)} %bitcast.19), custom_call_target="tpu_custom_call" | custom-call | flops 400000000 | bytes 4000000 | tf_op jit(solution)/shard_map/pallas_call | solution.py:341
  102.8 0.0 collective-permute-done.1
  102.8 2.5 %add_convert_fusion = bf16[4,192,512]{2,1,0:T(8,128)(2,1)} fusion(bf16[4,192,512]{2,1,0:T(8,128)(2,1)} %collective-permute-done.1, bf16[4,192,512]{2,1,0:T(8,128)(2,1)} %shard_map.114), kind=kLoop, calls=%fused_computation | loop fusion | flops 1572864 | bytes 2359296 | tf_op jit(solution)/shard_map/convert_element_type | solution.py:349
  105.3 5.1 %all-to-all-start.2 = ((bf16[4,192,512]{2,1,0:T(8,128)(2,1)}), bf16[4,192,512]{2,1,0:T(8,128)(2,1)}, u32[]{:S(2)}, u32[]{:S(2)}) async-start(bf16[4,192,512]{2,1,0:T(8,128)(2,1)} %add_convert_fusion), calls=%async_computation.2 | async-start | bytes 1572864 | tf_op jit(solution)/shard_map/all_to_all | solution.py:350
  110.4 2.0 %collective-permute-start.4 = (bf16[8,192,128]{2,1,0:T(8,128)(2,1)}, bf16[8,192,128]{2,1,0:T(8,128)(2,1)}, u32[]{:S(2)}, u32[]{:S(2)}) collective-permute-start(bf16[8,192,128]{2,1,0:T(8,128)(2,1)} %all_to_all.21), channel_id=1, source_target_pairs={{0,4},{1,5},{2,6},{3,7},{4,0},{5,1},{6,2},{7,3},{8,12},{9,13},{10,... | collective-permute-start | bytes 1179656 | tf_op jit(solution)/shard_map/ppermute | solution.py:320
  112.3 0.0 collective-permute-done.2.side_hbm
  112.3 2.8 %collective-permute-start.3 = (bf16[2,8,192,128]{3,2,1,0:T(8,128)(2,1)}, bf16[2,8,192,128]{3,2,1,0:T(8,128)(2,1)}, u32[]{:S(2)}, u32[]{:S(2)}) collective-permute-start(bf16[2,8,192,128]{3,2,1,0:T(8,128)(2,1)} %collective-permute-done.2.side_hbm), channel_id=1, source_target_pairs={{0,1},{1,0},{2,3},{3,2},{4,5},{5,4},{6,7},{7,6},{8,9},{9,8},{10,11... | collective-permute-start | bytes 2359304 | tf_op jit(solution)/shard_map/ppermute | solution.py:336
  115.2 14.3 %all-to-all-done.2.parts_ref = bf16[4,192,512]{2,1,0:T(8,128)(2,1)} async-done(((bf16[4,192,512]{2,1,0:T(8,128)(2,1)}), bf16[4,192,512]{2,1,0:T(8,128)(2,1)}, u32[]{:S(2)}, u32[]{:S(2)}) %all-to-all-start.2) | async-done | bytes 786464 | tf_op jit(solution)/shard_map/all_to_all | solution.py:350
  129.4 2.1 %shard_map.115 = bf16[16,24,256]{2,1,0:T(8,128)(2,1)} custom-call(bf16[4,192,512]{2,1,0:T(8,128)(2,1)} %all-to-all-done.2.parts_ref), custom_call_target="tpu_custom_call" | custom-call | flops 10000000 | bytes 1800000 | tf_op jit(solution)/shard_map/pallas_call | solution.py:353
  131.5 13.3 %all-to-all-start.3 = ((bf16[16,24,256]{2,1,0:T(8,128)(2,1)}), bf16[16,24,256]{2,1,0:T(8,128)(2,1)}, u32[]{:S(2)}, u32[]{:S(2)}) async-start(bf16[16,24,256]{2,1,0:T(8,128)(2,1)} %shard_map.115), calls=%async_computation.3 | async-start | bytes 393216 | tf_op jit(solution)/shard_map/all_to_all | solution.py:354
  144.8 0.0 collective-permute-done.4.far_hbm
  144.8 1.9 %collective-permute-start.5 = (bf16[8,192,128]{2,1,0:T(8,128)(2,1)}, bf16[8,192,128]{2,1,0:T(8,128)(2,1)}, u32[]{:S(2)}, u32[]{:S(2)}) collective-permute-start(bf16[8,192,128]{2,1,0:T(8,128)(2,1)} %collective-permute-done.4.far_hbm), channel_id=1, source_target_pairs={{0,1},{1,0},{2,3},{3,2},{4,5},{5,4},{6,7},{7,6},{8,9},{9,8},{10,11... | collective-permute-start | bytes 1179656 | tf_op jit(solution)/shard_map/ppermute | solution.py:337
  146.7 2.0 %collective-permute-done.5.far2_hbm = bf16[8,192,128]{2,1,0:T(8,128)(2,1)} collective-permute-done((bf16[8,192,128]{2,1,0:T(8,128)(2,1)}, bf16[8,192,128]{2,1,0:T(8,128)(2,1)}, u32[]{:S(2)}, u32[]{:S(2)}) %collective-permute-start.5) | collective-permute-done | bytes 393248 | tf_op jit(solution)/shard_map/ppermute | solution.py:337
  148.8 0.0 collective-permute-done.3.side2_hbm
  148.8 0.0 all-gather.5.cloned.1.call-done.delta_ref
  148.8 5.7 %shard_map.116 = (bf16[512,256]{1,0:T(8,128)(2,1)}, bf16[512,256]{1,0:T(8,128)(2,1)}, bf16[256,512]{1,0:T(8,128)(2,1)}) custom-call(s32[1]{0:T(128)} %bitcast.2.t_ref, bf16[1536,768]{1,0:T(8,128)(2,1)} %all-gather.5.cloned.1.call-done.delta_ref, bf16[2,8,192,128]{3,2,1,0:T(8,128)(2,1)} %pad_maximum_fusion.pair_hbm, ...), custom_call_target="tpu_custom_call" | custom-call | flops 1200000000 | bytes 6000000 | tf_op jit(solution)/shard_map/pallas_call | solution.py:355
  154.5 6.9 %all-to-all-done.3 = bf16[16,24,256]{2,1,0:T(8,128)(2,1)} async-done(((bf16[16,24,256]{2,1,0:T(8,128)(2,1)}), bf16[16,24,256]{2,1,0:T(8,128)(2,1)}, u32[]{:S(2)}, u32[]{:S(2)}) %all-to-all-start.3) | async-done | bytes 196640 | tf_op jit(solution)/shard_map/all_to_all | solution.py:354
  161.3 1.9 %shard_map.117 = bf16[128,512]{1,0:T(8,128)(2,1)} custom-call(s32[2,128]{1,0:T(2,128)} %bitcast.26, s32[2,128]{1,0:T(2,128)} %bitcast.28, bf16[384,256]{1,0:T(8,128)(2,1)} %bitcast.12.ret_ref), custom_call_target="tpu_custom_call" | custom-call | flops 50000000 | bytes 400000 | tf_op jit(solution)/shard_map/pallas_call | solution.py:364
Async XLA Ops:
  7.2 76.8 %all-gather.3.cloned.1.call-start = ((), (), s32[]{:S(2)}) async-start(), calls=%async_computation.4 | async-start | bytes 3538944 | tf_op jit(solution)/shard_map/all_gather | solution.py:311
  50.3 98.4 %all-gather.5.cloned.1.call-start = ((), (), s32[]{:S(2)}) async-start(), calls=%async_computation.5 | async-start | bytes 2654208 | tf_op jit(solution)/shard_map/all_gather | solution.py:338
  72.8 3.8 %collective-permute-start = (bf16[8,192,128]{2,1,0:T(8,128)(2,1)}, bf16[8,192,128]{2,1,0:T(8,128)(2,1)S(1)}, u32[]{:S(2)}, u32[]{:S(2)}) collective-permute-start(bf16[8,192,128]{2,1,0:T(8,128)(2,1)} %all_to_all.21), channel_id=1, source_target_pairs={{0,1},{1,0},{2,3},{3,2},{4,5},{5,4},{6,7},{7,6},{8,9},{9,8},{10,11... | collective-permute-start | bytes 1179656 | tf_op jit(solution)/shard_map/ppermute | solution.py:317
  93.0 9.9 %collective-permute-start.1 = (bf16[4,192,512]{2,1,0:T(8,128)(2,1)}, bf16[4,192,512]{2,1,0:T(8,128)(2,1)}, u32[]{:S(2)}, u32[]{:S(2)}) collective-permute-start(bf16[4,192,512]{2,1,0:T(8,128)(2,1)} %get-tuple-element.15), channel_id=1, source_target_pairs={{0,1},{1,0},{2,3},{3,2},{4,5},{5,4},{6,7},{7,6},{8,9},{9,8},{10,11... | collective-permute-start | bytes 2359304 | tf_op jit(solution)/shard_map/ppermute | solution.py:340
  95.1 17.2 %collective-permute-start.2 = (bf16[2,8,192,128]{3,2,1,0:T(8,128)(2,1)}, bf16[2,8,192,128]{3,2,1,0:T(8,128)(2,1)}, u32[]{:S(2)}, u32[]{:S(2)}) collective-permute-start(bf16[2,8,192,128]{3,2,1,0:T(8,128)(2,1)} %pad_maximum_fusion.pair_hbm), channel_id=1, source_target_pairs={{0,2},{1,7},{2,4},{3,1},{4,6},{5,3},{6,0},{7,5},{8,10},{9,15},{10,... | collective-permute-start | bytes 2359304 | tf_op jit(solution)/shard_map/ppermute | solution.py:319
  105.3 24.1 %all-to-all-start.2 = ((bf16[4,192,512]{2,1,0:T(8,128)(2,1)}), bf16[4,192,512]{2,1,0:T(8,128)(2,1)}, u32[]{:S(2)}, u32[]{:S(2)}) async-start(bf16[4,192,512]{2,1,0:T(8,128)(2,1)} %add_convert_fusion), calls=%async_computation.2 | async-start | bytes 1572864 | tf_op jit(solution)/shard_map/all_to_all | solution.py:350
  110.4 34.4 %collective-permute-start.4 = (bf16[8,192,128]{2,1,0:T(8,128)(2,1)}, bf16[8,192,128]{2,1,0:T(8,128)(2,1)}, u32[]{:S(2)}, u32[]{:S(2)}) collective-permute-start(bf16[8,192,128]{2,1,0:T(8,128)(2,1)} %all_to_all.21), channel_id=1, source_target_pairs={{0,4},{1,5},{2,6},{3,7},{4,0},{5,1},{6,2},{7,3},{8,12},{9,13},{10,... | collective-permute-start | bytes 1179656 | tf_op jit(solution)/shard_map/ppermute | solution.py:320
  112.3 36.4 %collective-permute-start.3 = (bf16[2,8,192,128]{3,2,1,0:T(8,128)(2,1)}, bf16[2,8,192,128]{3,2,1,0:T(8,128)(2,1)}, u32[]{:S(2)}, u32[]{:S(2)}) collective-permute-start(bf16[2,8,192,128]{3,2,1,0:T(8,128)(2,1)} %collective-permute-done.2.side_hbm), channel_id=1, source_target_pairs={{0,1},{1,0},{2,3},{3,2},{4,5},{5,4},{6,7},{7,6},{8,9},{9,8},{10,11... | collective-permute-start | bytes 2359304 | tf_op jit(solution)/shard_map/ppermute | solution.py:336
  131.5 29.8 %all-to-all-start.3 = ((bf16[16,24,256]{2,1,0:T(8,128)(2,1)}), bf16[16,24,256]{2,1,0:T(8,128)(2,1)}, u32[]{:S(2)}, u32[]{:S(2)}) async-start(bf16[16,24,256]{2,1,0:T(8,128)(2,1)} %shard_map.115), calls=%async_computation.3 | async-start | bytes 393216 | tf_op jit(solution)/shard_map/all_to_all | solution.py:354
  144.8 4.0 %collective-permute-start.5 = (bf16[8,192,128]{2,1,0:T(8,128)(2,1)}, bf16[8,192,128]{2,1,0:T(8,128)(2,1)}, u32[]{:S(2)}, u32[]{:S(2)}) collective-permute-start(bf16[8,192,128]{2,1,0:T(8,128)(2,1)} %collective-permute-done.4.far_hbm), channel_id=1, source_target_pairs={{0,1},{1,0},{2,3},{3,2},{4,5},{5,4},{6,7},{7,6},{8,9},{9,8},{10,11... | collective-permute-start | bytes 1179656 | tf_op jit(solution)/shard_map/ppermute | solution.py:337
Sparse Core Ops, SparseCore 0:
  50.5 33.4 all-gather.2
  93.1 50.4 all-gather.4

commit v3 on v0

--- a/solution.py
+++ b/solution.py
@@ -172,28 +172,29 @@
     out_ref[:, 512:768] = (act * up).astype(BF)
 
 
-def slot_kernel(delta_ref, wg_hbm, wu_hbm, out_ref, wg, wu, sem):
+def slot_kernel(core_ref, own_ref, other_ref, wg_hbm, wu_hbm, wg2_hbm, wu2_hbm, out_ref, w, sem):
     copies = [
         [
-            pltpu.make_async_copy(src.at[k], dst.at[k], sem.at[side, k])
-            for side, (src, dst) in enumerate(((wg_hbm, wg), (wu_hbm, wu)))
+            pltpu.make_async_copy(
+                src.at[2 * i + core_ref[0]], w.at[i, :, pl.ds(part * 256, 256)], sem.at[i, part]
+            )
+            for part, src in enumerate((wg_hbm, wu_hbm, wg2_hbm, wu2_hbm))
         ]
-        for k in range(8)
+        for i in range(4)
     ]
     for group in copies:
         for copy in group:
             copy.start()
-    for k in range(8):
-        for copy in copies[k]:
+    deltas = jnp.concatenate([own_ref[:, 0:512], other_ref[:, 0:512]], axis=1)
+    for i in range(4):
+        for copy in copies[i]:
             copy.wait()
-        w = jnp.concatenate([wg[k].reshape(512, 256), wu[k].reshape(512, 256)], axis=1)
-        term = lax.dot_general(delta_ref[:, 0:512], w, LAST, preferred_element_type=F32)
-        out_ref[k] = term.astype(BF)
+        out_ref[i] = lax.dot_general(deltas, w[i], LAST, preferred_element_type=F32).astype(BF)
 
 
 def pack_kernel(parts_ref, out_ref):
     total = parts_ref[0].astype(F32)
-    for t in range(1, 8):
+    for t in range(1, 4):
         total = total + parts_ref[t].astype(F32)
     rows = total.astype(BF)
     rest = jnp.zeros((128, 256), F32)
@@ -253,7 +254,7 @@
     ).astype(BF)
 
 
-def call(kernel, out, specs, scratch=(), flops=0, size=0):
+def call(kernel, out, specs, scratch=(), flops=0, size=0, limit=67_043_328):
     single = not isinstance(out, (list, tuple))
     return pl.pallas_call(
         kernel,
@@ -262,7 +263,7 @@
         out_specs=VM if single else [VM] * len(out),
         scratch_shapes=scratch,
         cost_estimate=pl.CostEstimate(flops=flops, bytes_accessed=size, transcendentals=0),
-        compiler_params=pltpu.CompilerParams(vmem_limit_bytes=67_043_328),
+        compiler_params=pltpu.CompilerParams(vmem_limit_bytes=limit),
     )
 
 
@@ -297,7 +298,10 @@
     pair = jnp.concatenate([mine[None], turned[None]], axis=0)
     side = lax.ppermute(pair, "tensor", SIDE)
     far = lax.ppermute(mine, "tensor", FAR)
+    gate2 = lax.ppermute(gate_weight, "tensor", SWAP)
+    up2 = lax.ppermute(up_weight, "tensor", SWAP)
     whole, pair = lax.optimization_barrier((whole, pair))
+    core = lax.bitwise_and(t, 1)
     delta = call(
         forward_kernel,
         shape((192, 768)),
@@ -316,15 +320,19 @@
     far2 = lax.ppermute(far, "tensor", SWAP)
     deltas = lax.all_gather(delta, "dp", axis=0, tiled=True)
 
+    delta2 = lax.ppermute(delta, "tensor", SWAP)
+    blocks = (8, 512, 256)
     terms = call(
         slot_kernel,
-        shape((8, 192, 512)),
-        [VM, HB, HB],
-        [pltpu.VMEM((8, 4, 128, 256), BF), pltpu.VMEM((8, 4, 128, 256), BF), dma((2, 8))],
+        shape((4, 192, 512)),
+        [SM, VM, VM, HB, HB, HB, HB],
+        [pltpu.VMEM((4, 512, 1024), BF), dma((4, 4))],
         flops=800_000_000,
         size=6_000_000,
-    )(delta, wg, wu)
-    parts = lax.all_to_all(terms, "tensor", 0, 0, tiled=True)
+    )(core, delta, delta2, *(w.reshape(blocks) for w in (gate_weight, up_weight, gate2, up2)))
+    parts = lax.all_to_all(
+        terms, "tensor", 0, 0, axis_index_groups=[[0, 2, 4, 6], [1, 3, 5, 7]], tiled=True
+    )
     back = call(pack_kernel, shape((16, 24, 256)), [VM], flops=10_000_000, size=1_800_000)(parts)
     returned = lax.all_to_all(back, "expert", 0, 0, tiled=True)
     gate_grad, up_grad, down_grad = call(

time: 180 us -> 169 us (0.939)
  the two profiles are of different devices: /device:TPU:1 before, /device:TPU:4 now
where the time goes in v3:
time: 169 us; the launch traced here: 168 us
  blocking collectives  61.8 us (37%)
  starting transfers between devices  36.6 us (22%)
  waiting for transfers between devices  28.8 us (17%)
  Pallas kernels  25.8 us (15%)
  between operations  14.2 us (8%)
    all_to_all x1, blocking collectives, layer(): lax.all_to_all(sent.reshape(16, 24, 512), 'expert', 0, 0, tiled=True)  42.8 us
    all_to_all x1, blocking collectives, layer(): mine = lax.all_to_all(corner, 'dp', 0, 0, tiled=True)  19 us
    all_to_all x1, waiting for transfers between devices, layer(): lax.all_to_all(terms, 'tensor', 0, 0, axis_index_groups=[[0, 2, 4, 6], [1...  14.7 us
    all_to_all x1, starting transfers between devices, layer(): returned = lax.all_to_all(back, 'expert', 0, 0, tiled=True)  12.6 us
    all_gather x1, waiting for transfers between devices, layer(): lax.all_gather(block.reshape(384, 512), 'tensor', axis=0, tiled=True)  6.26 us
    pallas_call x1, Pallas kernels, layer(): call(forward_kernel, shape((192, 768)), [HB, HB, HB, HB], [pltpu.VMEM((8,...  6.13 us
    pallas_call x1, Pallas kernels, layer(): call(weight_kernel, [shape((512, 256)), shape((512, 256)), shape((256, 51...  5.67 us
    all_to_all x1, starting transfers between devices, layer(): lax.all_to_all(terms, 'tensor', 0, 0, axis_index_groups=[[0, 2, 4, 6], [1...  5.47 us
  transfers between devices with their start and end apart: 12, of which 5 were waited for; matrix products, arithmetic and copies ran while one was open for 1% of the time, Pallas kernels for 9%

profile of v3, /device:TPU:4, one launch (start us, length us, event | category | flops | bytes accessed | tf_op | source)
XLA Modules:
  0.0 168.1 jit_solution(9903858958534017348)
XLA Ops:
  7.2 0.0 all-gather.3.cloned.1.call-start
  7.2 2.7 %shard_map.111 = bf16[384,512]{1,0:T(8,128)(2,1)} custom-call(s32[1]{0:T(128)} %bitcast.2.t_ref, s32[2,128]{1,0:T(2,128)} %bitcast.30, s32[2,128]{1,0:T(2,128)} %bitcast.32, f32[2,128]{1,0:T(2,128)} %bitcast.34, bf16[128,4096]{1,0:T(8,128)(2,1)} %tok_hbm.1, bf16[128,4096]{1,0:T(8,128)(2,1)} %grad_hbm.1), custom_call_target="tpu_custom_call" | custom-call | flops 100000000 | bytes 700000 | tf_op jit(solution)/shard_map/pallas_call | solution.py:282
  10.0 42.8 %all_to_all.20.block_ref = bf16[16,24,512]{2,1,0:T(8,128)(2,1)} all-to-all(bf16[16,24,512]{2,1,0:T(8,128)(2,1)} %bitcast.28), channel_id=1, replica_groups=mesh['expert'=16,'dp'=8,'tensor'=8] {'expert'}, dimensions={0} | all-to-all | bytes 786432 | tf_op jit(solution)/shard_map/all_to_all | solution.py:290
  52.7 0.0 all-gather.3.cloned.1.call-update
  52.8 0.0 all-gather.5.cloned.1.call-start
  52.8 1.9 %shard_map.112 = bf16[8,192,128]{2,1,0:T(8,128)(2,1)} custom-call(bf16[16,24,512]{2,1,0:T(8,128)(2,1)} %all_to_all.20.block_ref), custom_call_target="tpu_custom_call" | custom-call | flops 20000000 | bytes 800000 | tf_op jit(solution)/shard_map/pallas_call | solution.py:293
  54.7 19.0 %all_to_all.21 = bf16[8,192,128]{2,1,0:T(8,128)(2,1)S(1)} all-to-all(bf16[8,192,128]{2,1,0:T(8,128)(2,1)} %shard_map.112), channel_id=1, replica_groups=mesh['expert'=16,'dp'=8,'tensor'=8] {'dp'}, dimensions={0} | all-to-all | bytes 786432 | tf_op jit(solution)/shard_map/all_to_all | solution.py:296
  73.7 0.0 copy-start
  73.7 1.9 %collective-permute-start = (bf16[8,192,128]{2,1,0:T(8,128)(2,1)S(1)}, bf16[8,192,128]{2,1,0:T(8,128)(2,1)S(1)}, u32[]{:S(2)}, u32[]{:S(2)}) collective-permute-start(bf16[8,192,128]{2,1,0:T(8,128)(2,1)S(1)} %all_to_all.21), channel_id=1, source_target_pairs={{0,1},{1,0},{2,3},{3,2},{4,5},{5,4},{6,7},{7,6},{8,9},{9,8},{10,11... | collective-permute-start | bytes 1179656 | tf_op jit(solution)/shard_map/ppermute | solution.py:297
  75.7 1.9 %collective-permute-done = bf16[8,192,128]{2,1,0:T(8,128)(2,1)S(1)} collective-permute-done((bf16[8,192,128]{2,1,0:T(8,128)(2,1)S(1)}, bf16[8,192,128]{2,1,0:T(8,128)(2,1)S(1)}, u32[]{:S(2)}, u32[]{:S(2)}) %collective-permute-start) | collective-permute-done | bytes 393248 | tf_op jit(solution)/shard_map/ppermute | solution.py:297
  77.6 0.0 copy-done
  77.6 0.9 pad_maximum_fusion.pair_hbm
  78.5 6.3 %all-gather.3.cloned.1.call-done = bf16[3072,512]{1,0:T(8,128)(2,1)} async-done(((bf16[384,512]{1,0:T(8,128)(2,1)}), bf16[3072,512]{1,0:T(8,128)(2,1)}) %all-gather.3.cloned.1.call-update) | async-done | bytes 3145744 | tf_op jit(solution)/shard_map/all_gather | solution.py:291
  84.8 6.1 %shard_map.113.own_ref = bf16[192,768]{1,0:T(8,128)(2,1)} custom-call(bf16[8,16,24,512]{3,2,1,0:T(8,128)(2,1)} %bitcast.25, bf16[8,4,128,256]{3,2,1,0:T(8,128)(2,1)} %bitcast.20, bf16[8,4,128,256]{3,2,1,0:T(8,128)(2,1)} %bitcast.22, bf16[256,4096]{1,0:T(8,128)(2,1)} %bitcast.26), custom_call_target="tpu_custom_call" | custom-call | flops 1300000000 | bytes 10000000 | tf_op jit(solution)/shard_map/pallas_call | solution.py:305
  90.9 0.0 all-gather.5.cloned.1.call-update
  90.9 2.1 %collective-permute-start.2 = (bf16[1,4096,256]{2,1,0:T(8,128)(2,1)}, bf16[1,4096,256]{2,1,0:T(8,128)(2,1)}, u32[]{:S(2)}, u32[]{:S(2)}) collective-permute-start(bf16[1,4096,256]{2,1,0:T(8,128)(2,1)} %param.13), channel_id=1, source_target_pairs={{0,1},{1,0},{2,3},{3,2},{4,5},{5,4},{6,7},{7,6},{8,9},{9,8},{10,11... | collective-permute-start | bytes 6291464 | tf_op jit(solution)/shard_map/ppermute | solution.py:301
  93.1 2.2 %collective-permute-start.3 = (bf16[1,4096,256]{2,1,0:T(8,128)(2,1)}, bf16[1,4096,256]{2,1,0:T(8,128)(2,1)}, u32[]{:S(2)}, u32[]{:S(2)}) collective-permute-start(bf16[1,4096,256]{2,1,0:T(8,128)(2,1)} %param.14), channel_id=1, source_target_pairs={{0,1},{1,0},{2,3},{3,2},{4,5},{5,4},{6,7},{7,6},{8,9},{9,8},{10,11... | collective-permute-start | bytes 6291464 | tf_op jit(solution)/shard_map/ppermute | solution.py:302
  95.3 2.1 %collective-permute-start.1 = (bf16[192,768]{1,0:T(8,128)(2,1)}, bf16[192,768]{1,0:T(8,128)(2,1)}, u32[]{:S(2)}, u32[]{:S(2)}) collective-permute-start(bf16[192,768]{1,0:T(8,128)(2,1)} %shard_map.113.own_ref), channel_id=1, source_target_pairs={{0,1},{1,0},{2,3},{3,2},{4,5},{5,4},{6,7},{7,6},{8,9},{9,8},{10,11... | collective-permute-start | bytes 884744 | tf_op jit(solution)/shard_map/ppermute | solution.py:323
  97.4 3.8 %collective-permute-start.4 = (bf16[2,8,192,128]{3,2,1,0:T(8,128)(2,1)}, bf16[2,8,192,128]{3,2,1,0:T(8,128)(2,1)}, u32[]{:S(2)}, u32[]{:S(2)}) collective-permute-start(bf16[2,8,192,128]{3,2,1,0:T(8,128)(2,1)} %pad_maximum_fusion.pair_hbm), channel_id=1, source_target_pairs={{0,2},{1,7},{2,4},{3,1},{4,6},{5,3},{6,0},{7,5},{8,10},{9,15},{10,... | collective-permute-start | bytes 2359304 | tf_op jit(solution)/shard_map/ppermute | solution.py:299
  101.3 0.0 collective-permute-done.2
  101.3 0.0 collective-permute-done.3
  101.3 0.0 collective-permute-done.1.other_ref
  101.3 5.3 %shard_map.114 = bf16[4,192,512]{2,1,0:T(8,128)(2,1)} custom-call(s32[1]{0:T(128)S(6)} %and.4.core_ref, bf16[192,768]{1,0:T(8,128)(2,1)} %shard_map.113.own_ref, bf16[192,768]{1,0:T(8,128)(2,1)} %collective-permute-done.1.other_ref, bf16[8,512,256]{2,1,0:T(8,128)(2,1)} %bitcast.21, bf16[8,512,256]{2,1,0:T(8,128)(2,1)} %bitcast.23, ...), custom_call_target="tpu_custom_call" | custom-call | flops 800000000 | bytes 6000000 | tf_op jit(solution)/shard_map/pallas_call | solution.py:325
  106.7 5.5 %all-to-all-start.2 = ((bf16[4,192,512]{2,1,0:T(8,128)(2,1)}), bf16[4,192,512]{2,1,0:T(8,128)(2,1)}, u32[]{:S(2)}, u32[]{:S(2)}) async-start(bf16[4,192,512]{2,1,0:T(8,128)(2,1)} %shard_map.114), calls=%async_computation.2 | async-start | bytes 1572864 | tf_op jit(solution)/shard_map/all_to_all | solution.py:333
  112.1 2.0 %collective-permute-start.6 = (bf16[8,192,128]{2,1,0:T(8,128)(2,1)}, bf16[8,192,128]{2,1,0:T(8,128)(2,1)}, u32[]{:S(2)}, u32[]{:S(2)}) collective-permute-start(bf16[8,192,128]{2,1,0:T(8,128)(2,1)} %copy-done), channel_id=1, source_target_pairs={{0,4},{1,5},{2,6},{3,7},{4,0},{5,1},{6,2},{7,3},{8,12},{9,13},{10,... | collective-permute-start | bytes 1179656 | tf_op jit(solution)/shard_map/ppermute | solution.py:300
  114.1 0.0 collective-permute-done.4.side_hbm
  114.1 2.4 %collective-permute-start.5 = (bf16[2,8,192,128]{3,2,1,0:T(8,128)(2,1)}, bf16[2,8,192,128]{3,2,1,0:T(8,128)(2,1)}, u32[]{:S(2)}, u32[]{:S(2)}) collective-permute-start(bf16[2,8,192,128]{3,2,1,0:T(8,128)(2,1)} %collective-permute-done.4.side_hbm), channel_id=1, source_target_pairs={{0,1},{1,0},{2,3},{3,2},{4,5},{5,4},{6,7},{7,6},{8,9},{9,8},{10,11... | collective-permute-start | bytes 2359304 | tf_op jit(solution)/shard_map/ppermute | solution.py:319
  116.5 14.7 %all-to-all-done.2.parts_ref = bf16[4,192,512]{2,1,0:T(8,128)(2,1)} async-done(((bf16[4,192,512]{2,1,0:T(8,128)(2,1)}), bf16[4,192,512]{2,1,0:T(8,128)(2,1)}, u32[]{:S(2)}, u32[]{:S(2)}) %all-to-all-start.2) | async-done | bytes 786464 | tf_op jit(solution)/shard_map/all_to_all | solution.py:333
  131.2 2.0 %shard_map.115 = bf16[16,24,256]{2,1,0:T(8,128)(2,1)} custom-call(bf16[4,192,512]{2,1,0:T(8,128)(2,1)} %all-to-all-done.2.parts_ref), custom_call_target="tpu_custom_call" | custom-call | flops 10000000 | bytes 1800000 | tf_op jit(solution)/shard_map/pallas_call | solution.py:336
  133.2 12.6 %all-to-all-start.3 = ((bf16[16,24,256]{2,1,0:T(8,128)(2,1)}), bf16[16,24,256]{2,1,0:T(8,128)(2,1)}, u32[]{:S(2)}, u32[]{:S(2)}) async-start(bf16[16,24,256]{2,1,0:T(8,128)(2,1)} %shard_map.115), calls=%async_computation.3 | async-start | bytes 393216 | tf_op jit(solution)/shard_map/all_to_all | solution.py:337
  145.8 0.0 collective-permute-done.6.far_hbm
  145.8 1.9 %collective-permute-start.7 = (bf16[8,192,128]{2,1,0:T(8,128)(2,1)}, bf16[8,192,128]{2,1,0:T(8,128)(2,1)}, u32[]{:S(2)}, u32[]{:S(2)}) collective-permute-start(bf16[8,192,128]{2,1,0:T(8,128)(2,1)} %collective-permute-done.6.far_hbm), channel_id=1, source_target_pairs={{0,1},{1,0},{2,3},{3,2},{4,5},{5,4},{6,7},{7,6},{8,9},{9,8},{10,11... | collective-permute-start | bytes 1179656 | tf_op jit(solution)/shard_map/ppermute | solution.py:320
  147.8 2.0 %collective-permute-done.7.far2_hbm = bf16[8,192,128]{2,1,0:T(8,128)(2,1)} collective-permute-done((bf16[8,192,128]{2,1,0:T(8,128)(2,1)}, bf16[8,192,128]{2,1,0:T(8,128)(2,1)}, u32[]{:S(2)}, u32[]{:S(2)}) %collective-permute-start.7) | collective-permute-done | bytes 393248 | tf_op jit(solution)/shard_map/ppermute | solution.py:320
  149.8 0.0 collective-permute-done.5.side2_hbm
  149.8 0.0 all-gather.5.cloned.1.call-done.delta_ref
  149.8 5.7 %shard_map.116 = (bf16[512,256]{1,0:T(8,128)(2,1)}, bf16[512,256]{1,0:T(8,128)(2,1)}, bf16[256,512]{1,0:T(8,128)(2,1)}) custom-call(s32[1]{0:T(128)} %bitcast.2.t_ref, bf16[1536,768]{1,0:T(8,128)(2,1)} %all-gather.5.cloned.1.call-done.delta_ref, bf16[2,8,192,128]{3,2,1,0:T(8,128)(2,1)} %pad_maximum_fusion.pair_hbm, ...), custom_call_target="tpu_custom_call" | custom-call | flops 1200000000 | bytes 6000000 | tf_op jit(solution)/shard_map/pallas_call | solution.py:338
  155.5 3.9 %all-to-all-done.3 = bf16[16,24,256]{2,1,0:T(8,128)(2,1)} async-done(((bf16[16,24,256]{2,1,0:T(8,128)(2,1)}), bf16[16,24,256]{2,1,0:T(8,128)(2,1)}, u32[]{:S(2)}, u32[]{:S(2)}) %all-to-all-start.3) | async-done | bytes 196640 | tf_op jit(solution)/shard_map/all_to_all | solution.py:337
  159.4 1.9 %shard_map.117 = bf16[128,512]{1,0:T(8,128)(2,1)} custom-call(s32[2,128]{1,0:T(2,128)} %bitcast.31, s32[2,128]{1,0:T(2,128)} %bitcast.33, bf16[384,256]{1,0:T(8,128)(2,1)} %bitcast.16.ret_ref), custom_call_target="tpu_custom_call" | custom-call | flops 50000000 | bytes 400000 | tf_op jit(solution)/shard_map/pallas_call | solution.py:347
Async XLA Ops:
  7.2 77.6 %all-gather.3.cloned.1.call-start = ((), (), s32[]{:S(2)}) async-start(), calls=%async_computation.4 | async-start | bytes 3538944 | tf_op jit(solution)/shard_map/all_gather | solution.py:291
  52.8 97.1 %all-gather.5.cloned.1.call-start = ((), (), s32[]{:S(2)}) async-start(), calls=%async_computation.5 | async-start | bytes 2654208 | tf_op jit(solution)/shard_map/all_gather | solution.py:321
  73.7 3.8 %copy-start = (bf16[8,192,128]{2,1,0:T(8,128)(2,1)}, bf16[8,192,128]{2,1,0:T(8,128)(2,1)S(1)}, u32[]{:S(2)}) copy-start(bf16[8,192,128]{2,1,0:T(8,128)(2,1)S(1)} %all_to_all.21) | copy-start | bytes 1179652
  73.7 3.8 %collective-permute-start = (bf16[8,192,128]{2,1,0:T(8,128)(2,1)S(1)}, bf16[8,192,128]{2,1,0:T(8,128)(2,1)S(1)}, u32[]{:S(2)}, u32[]{:S(2)}) collective-permute-start(bf16[8,192,128]{2,1,0:T(8,128)(2,1)S(1)} %all_to_all.21), channel_id=1, source_target_pairs={{0,1},{1,0},{2,3},{3,2},{4,5},{5,4},{6,7},{7,6},{8,9},{9,8},{10,11... | collective-permute-start | bytes 1179656 | tf_op jit(solution)/shard_map/ppermute | solution.py:297
  90.9 10.3 %collective-permute-start.2 = (bf16[1,4096,256]{2,1,0:T(8,128)(2,1)}, bf16[1,4096,256]{2,1,0:T(8,128)(2,1)}, u32[]{:S(2)}, u32[]{:S(2)}) collective-permute-start(bf16[1,4096,256]{2,1,0:T(8,128)(2,1)} %param.13), channel_id=1, source_target_pairs={{0,1},{1,0},{2,3},{3,2},{4,5},{5,4},{6,7},{7,6},{8,9},{9,8},{10,11... | collective-permute-start | bytes 6291464 | tf_op jit(solution)/shard_map/ppermute | solution.py:301
  93.1 8.2 %collective-permute-start.3 = (bf16[1,4096,256]{2,1,0:T(8,128)(2,1)}, bf16[1,4096,256]{2,1,0:T(8,128)(2,1)}, u32[]{:S(2)}, u32[]{:S(2)}) collective-permute-start(bf16[1,4096,256]{2,1,0:T(8,128)(2,1)} %param.14), channel_id=1, source_target_pairs={{0,1},{1,0},{2,3},{3,2},{4,5},{5,4},{6,7},{7,6},{8,9},{9,8},{10,11... | collective-permute-start | bytes 6291464 | tf_op jit(solution)/shard_map/ppermute | solution.py:302
  95.3 6.0 %collective-permute-start.1 = (bf16[192,768]{1,0:T(8,128)(2,1)}, bf16[192,768]{1,0:T(8,128)(2,1)}, u32[]{:S(2)}, u32[]{:S(2)}) collective-permute-start(bf16[192,768]{1,0:T(8,128)(2,1)} %shard_map.113.own_ref), channel_id=1, source_target_pairs={{0,1},{1,0},{2,3},{3,2},{4,5},{5,4},{6,7},{7,6},{8,9},{9,8},{10,11... | collective-permute-start | bytes 884744 | tf_op jit(solution)/shard_map/ppermute | solution.py:323
  97.4 16.7 %collective-permute-start.4 = (bf16[2,8,192,128]{3,2,1,0:T(8,128)(2,1)}, bf16[2,8,192,128]{3,2,1,0:T(8,128)(2,1)}, u32[]{:S(2)}, u32[]{:S(2)}) collective-permute-start(bf16[2,8,192,128]{3,2,1,0:T(8,128)(2,1)} %pad_maximum_fusion.pair_hbm), channel_id=1, source_target_pairs={{0,2},{1,7},{2,4},{3,1},{4,6},{5,3},{6,0},{7,5},{8,10},{9,15},{10,... | collective-permute-start | bytes 2359304 | tf_op jit(solution)/shard_map/ppermute | solution.py:299
  106.7 24.5 %all-to-all-start.2 = ((bf16[4,192,512]{2,1,0:T(8,128)(2,1)}), bf16[4,192,512]{2,1,0:T(8,128)(2,1)}, u32[]{:S(2)}, u32[]{:S(2)}) async-start(bf16[4,192,512]{2,1,0:T(8,128)(2,1)} %shard_map.114), calls=%async_computation.2 | async-start | bytes 1572864 | tf_op jit(solution)/shard_map/all_to_all | solution.py:333
  112.1 33.7 %collective-permute-start.6 = (bf16[8,192,128]{2,1,0:T(8,128)(2,1)}, bf16[8,192,128]{2,1,0:T(8,128)(2,1)}, u32[]{:S(2)}, u32[]{:S(2)}) collective-permute-start(bf16[8,192,128]{2,1,0:T(8,128)(2,1)} %copy-done), channel_id=1, source_target_pairs={{0,4},{1,5},{2,6},{3,7},{4,0},{5,1},{6,2},{7,3},{8,12},{9,13},{10,... | collective-permute-start | bytes 1179656 | tf_op jit(solution)/shard_map/ppermute | solution.py:300
  114.1 35.7 %collective-permute-start.5 = (bf16[2,8,192,128]{3,2,1,0:T(8,128)(2,1)}, bf16[2,8,192,128]{3,2,1,0:T(8,128)(2,1)}, u32[]{:S(2)}, u32[]{:S(2)}) collective-permute-start(bf16[2,8,192,128]{3,2,1,0:T(8,128)(2,1)} %collective-permute-done.4.side_hbm), channel_id=1, source_target_pairs={{0,1},{1,0},{2,3},{3,2},{4,5},{5,4},{6,7},{7,6},{8,9},{9,8},{10,11... | collective-permute-start | bytes 2359304 | tf_op jit(solution)/shard_map/ppermute | solution.py:319
  133.2 26.1 %all-to-all-start.3 = ((bf16[16,24,256]{2,1,0:T(8,128)(2,1)}), bf16[16,24,256]{2,1,0:T(8,128)(2,1)}, u32[]{:S(2)}, u32[]{:S(2)}) async-start(bf16[16,24,256]{2,1,0:T(8,128)(2,1)} %shard_map.115), calls=%async_computation.3 | async-start | bytes 393216 | tf_op jit(solution)/shard_map/all_to_all | solution.py:337
  145.8 4.0 %collective-permute-start.7 = (bf16[8,192,128]{2,1,0:T(8,128)(2,1)}, bf16[8,192,128]{2,1,0:T(8,128)(2,1)}, u32[]{:S(2)}, u32[]{:S(2)}) collective-permute-start(bf16[8,192,128]{2,1,0:T(8,128)(2,1)} %collective-permute-done.6.far_hbm), channel_id=1, source_target_pairs={{0,1},{1,0},{2,3},{3,2},{4,5},{5,4},{6,7},{7,6},{8,9},{9,8},{10,11... | collective-permute-start | bytes 1179656 | tf_op jit(solution)/shard_map/ppermute | solution.py:320
Sparse Core Ops, SparseCore 0:
  52.9 31.8 all-gather.2
  91.0 50.3 all-gather.4

commit v4 on v3

--- a/solution.py
+++ b/solution.py
@@ -95,7 +95,7 @@
     return jnp.concatenate([near, rest], axis=0)
 
 
-def forward_kernel(g_hbm, wg_hbm, wu_hbm, wd_hbm, out_ref, buf, wg, wu, wd, sem):
+def forward_kernel(g_hbm, wg_hbm, wu_hbm, wd_hbm, out_ref, buf, w, wd, sem):
     copies = [pltpu.make_async_copy(g_hbm.at[t], buf.at[t], sem.at[0, t]) for t in range(8)]
     down = [
         pltpu.make_async_copy(
@@ -106,9 +106,12 @@
     first = [
         [
             pltpu.make_async_copy(
-                src.at[pl.ds(q * 4, 4)], dst.at[pl.ds(q * 4, 4)], sem.at[2 + side, q]
+                src.at[pl.ds(q * 4, 4), unit],
+                w.at[q, unit, :, :, pl.ds(side * 256, 256)],
+                sem.at[2 + q, unit * 2 + side],
             )
-            for side, (src, dst) in enumerate(((wg_hbm, wg), (wu_hbm, wu)))
+            for unit in range(4)
+            for side, src in enumerate((wg_hbm, wu_hbm))
         ]
         for q in range(2)
     ]
@@ -135,7 +138,7 @@
     terms = []
     for q in range(2):
         down[q].wait()
-        w = jnp.concatenate(
+        wide = jnp.concatenate(
             [
                 wd[:, (q * 4 + j) * 512 + unit * 128 : (q * 4 + j) * 512 + (unit + 1) * 128]
                 for unit in range(4)
@@ -144,7 +147,7 @@
             axis=1,
         )
         terms.append(
-            lax.dot_general(rows(range(4, 8), q), w, LAST, preferred_element_type=F32)
+            lax.dot_general(rows(range(4, 8), q), wide, LAST, preferred_element_type=F32)
         )
     back = settle(*terms)
     for copy in copies[0:4]:
@@ -153,16 +156,11 @@
     for q in range(2):
         for copy in first[q]:
             copy.wait()
-        w = jnp.concatenate(
-            [
-                jnp.concatenate(
-                    [m[q * 4 : (q + 1) * 4, unit].reshape(512, 256) for unit in range(4)], axis=0
-                )
-                for m in (wg, wu)
-            ],
-            axis=1,
-        )
-        terms.append(jnp.dot(rows(range(4), q), w, preferred_element_type=F32))
+        terms.append(
+            jnp.dot(
+                rows(range(4), q), w[q].reshape(2048, 512), preferred_element_type=F32
+            )
+        )
     both = settle(*terms)
     gate, up = both[:, 0:256], both[:, 256:512]
     sig = jax.nn.sigmoid(gate)
@@ -252,6 +250,9 @@
     down_ref[...] = lax.dot_general(
         delta_ref[:, 512:768], grad, FIRST, preferred_element_type=F32
     ).astype(BF)
+
+
+ROOM = 67_043_328 - 16_000_000
 
 
 def call(kernel, out, specs, scratch=(), flops=0, size=0, limit=67_043_328):
@@ -308,16 +309,13 @@
         [HB, HB, HB, HB],
         [
             pltpu.VMEM((8, 16, 24, 512), BF),
-            pltpu.VMEM((8, 4, 128, 256), BF),
-            pltpu.VMEM((8, 4, 128, 256), BF),
+            pltpu.VMEM((2, 4, 4, 128, 512), BF),
             pltpu.VMEM((256, 4096), BF),
             dma((4, 8)),
         ],
         flops=1_300_000_000,
         size=10_000_000,
     )(whole.reshape(8, 16, 24, 512), wg, wu, wd)
-    side2 = lax.ppermute(side, "tensor", SWAP)
-    far2 = lax.ppermute(far, "tensor", SWAP)
     deltas = lax.all_gather(delta, "dp", axis=0, tiled=True)
 
     delta2 = lax.ppermute(delta, "tensor", SWAP)
@@ -329,11 +327,15 @@
         [pltpu.VMEM((4, 512, 1024), BF), dma((4, 4))],
         flops=800_000_000,
         size=6_000_000,
+        limit=ROOM,
     )(core, delta, delta2, *(w.reshape(blocks) for w in (gate_weight, up_weight, gate2, up2)))
     parts = lax.all_to_all(
         terms, "tensor", 0, 0, axis_index_groups=[[0, 2, 4, 6], [1, 3, 5, 7]], tiled=True
     )
-    back = call(pack_kernel, shape((16, 24, 256)), [VM], flops=10_000_000, size=1_800_000)(parts)
+    back = call(pack_kernel, shape((16, 24, 256)), [VM], flops=10_000_000, size=1_800_000, limit=32 << 20)(parts)
+    side, far, back = lax.optimization_barrier((side, far, back))
+    side2 = lax.ppermute(side, "tensor", SWAP)
+    far2 = lax.ppermute(far, "tensor", SWAP)
     returned = lax.all_to_all(back, "expert", 0, 0, tiled=True)
     gate_grad, up_grad, down_grad = call(
         weight_kernel,

time: 169 us -> 178 us (1.053)
  the two profiles are of different devices: /device:TPU:4 before, /device:TPU:1 now
where the time goes in v4:
time: 178 us; the launch traced here: 175 us
  blocking collectives  55.2 us (31%)
  starting transfers between devices  45.7 us (26%)
  waiting for transfers between devices  28.3 us (16%)
  Pallas kernels  23.6 us (13%)
  between operations  14.2 us (8%)
  local copies, waits for them, and re-layouts  7.15 us (4%)
    all_to_all x1, blocking collectives, layer(): lax.all_to_all(sent.reshape(16, 24, 512), 'expert', 0, 0, tiled=True)  37.6 us
    all_to_all x1, blocking collectives, layer(): mine = lax.all_to_all(corner, 'dp', 0, 0, tiled=True)  17.6 us
    all_to_all x1, starting transfers between devices, layer(): returned = lax.all_to_all(back, 'expert', 0, 0, tiled=True)  12.3 us
    ppermute x1, starting transfers between devices, layer(): turned = lax.ppermute(mine, 'tensor', SWAP)  9.97 us
    all_gather x1, waiting for transfers between devices, layer(): lax.all_gather(block.reshape(384, 512), 'tensor', axis=0, tiled=True)  7.83 us
    all_to_all x1, waiting for transfers between devices, layer(): lax.all_to_all(terms, 'tensor', 0, 0, axis_index_groups=[[0, 2, 4, 6], [1...  7.73 us
    ppermute x1, waiting for transfers between devices, layer(): far = lax.ppermute(mine, 'tensor', FAR)  7.52 us
    unnamed x20, local copies, waits for them, and re-layouts  7.15 us
  transfers between devices with their start and end apart: 12, of which 6 were waited for; matrix products, arithmetic and copies ran while one was open for 1% of the time, Pallas kernels for 7%

profile of v4, /device:TPU:1, one launch (start us, length us, event | category | flops | bytes accessed | tf_op | source)
XLA Modules:
  0.0 175.1 jit_solution(11733949503125802012)
XLA Ops:
  7.2 0.0 all-gather.3.cloned.1.call-start
  7.2 2.7 %shard_map.111 = bf16[384,512]{1,0:T(8,128)(2,1)} custom-call(s32[1]{0:T(128)} %bitcast.2.t_ref, s32[2,128]{1,0:T(2,128)} %bitcast.32, s32[2,128]{1,0:T(2,128)} %bitcast.34, f32[2,128]{1,0:T(2,128)} %bitcast.36, bf16[128,4096]{1,0:T(8,128)(2,1)} %tok_hbm.1, bf16[128,4096]{1,0:T(8,128)(2,1)} %grad_hbm.1), custom_call_target="tpu_custom_call" | custom-call | flops 100000000 | bytes 700000 | tf_op jit(solution)/shard_map/pallas_call | solution.py:283
  10.0 37.6 %all_to_all.20.block_ref = bf16[16,24,512]{2,1,0:T(8,128)(2,1)} all-to-all(bf16[16,24,512]{2,1,0:T(8,128)(2,1)} %bitcast.30), channel_id=1, replica_groups=mesh['expert'=16,'dp'=8,'tensor'=8] {'expert'}, dimensions={0} | all-to-all | bytes 786432 | tf_op jit(solution)/shard_map/all_to_all | solution.py:291
  47.6 0.0 all-gather.3.cloned.1.call-update
  47.6 0.0 all-gather.5.cloned.1.call-start
  47.7 1.9 %shard_map.112 = bf16[8,192,128]{2,1,0:T(8,128)(2,1)} custom-call(bf16[16,24,512]{2,1,0:T(8,128)(2,1)} %all_to_all.20.block_ref), custom_call_target="tpu_custom_call" | custom-call | flops 20000000 | bytes 800000 | tf_op jit(solution)/shard_map/pallas_call | solution.py:294
  49.6 17.6 %all_to_all.21 = bf16[8,192,128]{2,1,0:T(8,128)(2,1)S(1)} all-to-all(bf16[8,192,128]{2,1,0:T(8,128)(2,1)} %shard_map.112), channel_id=1, replica_groups=mesh['expert'=16,'dp'=8,'tensor'=8] {'dp'}, dimensions={0} | all-to-all | bytes 786432 | tf_op jit(solution)/shard_map/all_to_all | solution.py:297
  67.1 0.0 copy-start.4
  67.1 10.0 %collective-permute-start = (bf16[8,192,128]{2,1,0:T(8,128)(2,1)S(1)}, bf16[8,192,128]{2,1,0:T(8,128)(2,1)S(1)}, u32[]{:S(2)}, u32[]{:S(2)}) collective-permute-start(bf16[8,192,128]{2,1,0:T(8,128)(2,1)S(1)} %all_to_all.21), channel_id=1, source_target_pairs={{0,1},{1,0},{2,3},{3,2},{4,5},{5,4},{6,7},{7,6},{8,9},{9,8},{10,11... | collective-permute-start | bytes 1179656 | tf_op jit(solution)/shard_map/ppermute | solution.py:298
  77.1 1.5 collective-permute-done
  78.6 0.0 copy-done.4
  78.6 0.9 pad_maximum_fusion.pair_hbm
  79.5 7.8 %all-gather.3.cloned.1.call-done = bf16[3072,512]{1,0:T(8,128)(2,1)} async-done(((bf16[384,512]{1,0:T(8,128)(2,1)}), bf16[3072,512]{1,0:T(8,128)(2,1)}) %all-gather.3.cloned.1.call-update) | async-done | bytes 3145744 | tf_op jit(solution)/shard_map/all_gather | solution.py:292
  87.4 6.2 %shard_map.113.own_ref = bf16[192,768]{1,0:T(8,128)(2,1)} custom-call(bf16[8,16,24,512]{3,2,1,0:T(8,128)(2,1)} %bitcast.25, bf16[8,4,128,256]{3,2,1,0:T(8,128)(2,1)} %bitcast.20, bf16[8,4,128,256]{3,2,1,0:T(8,128)(2,1)} %bitcast.22, bf16[256,4096]{1,0:T(8,128)(2,1)} %bitcast.26), custom_call_target="tpu_custom_call" | custom-call | flops 1300000000 | bytes 10000000 | tf_op jit(solution)/shard_map/pallas_call | solution.py:306
  93.5 0.0 all-gather.5.cloned.1.call-update
  93.6 2.2 %collective-permute-start.4 = (bf16[1,4096,256]{2,1,0:T(8,128)(2,1)}, bf16[1,4096,256]{2,1,0:T(8,128)(2,1)S(1)}, u32[]{:S(2)}, u32[]{:S(2)}) collective-permute-start(bf16[1,4096,256]{2,1,0:T(8,128)(2,1)} %param.13), channel_id=1, source_target_pairs={{0,1},{1,0},{2,3},{3,2},{4,5},{5,4},{6,7},{7,6},{8,9},{9,8},{10,11... | collective-permute-start | bytes 6291464 | tf_op jit(solution)/shard_map/ppermute | solution.py:302
  95.8 2.1 %collective-permute-start.5 = (bf16[1,4096,256]{2,1,0:T(8,128)(2,1)}, bf16[1,4096,256]{2,1,0:T(8,128)(2,1)S(1)}, u32[]{:S(2)}, u32[]{:S(2)}) collective-permute-start(bf16[1,4096,256]{2,1,0:T(8,128)(2,1)} %param.14), channel_id=1, source_target_pairs={{0,1},{1,0},{2,3},{3,2},{4,5},{5,4},{6,7},{7,6},{8,9},{9,8},{10,11... | collective-permute-start | bytes 6291464 | tf_op jit(solution)/shard_map/ppermute | solution.py:303
  97.9 2.2 %collective-permute-start.3 = (bf16[192,768]{1,0:T(8,128)(2,1)}, bf16[192,768]{1,0:T(8,128)(2,1)S(1)}, u32[]{:S(2)}, u32[]{:S(2)}) collective-permute-start(bf16[192,768]{1,0:T(8,128)(2,1)} %shard_map.113.own_ref), channel_id=1, source_target_pairs={{0,1},{1,0},{2,3},{3,2},{4,5},{5,4},{6,7},{7,6},{8,9},{9,8},{10,11... | collective-permute-start | bytes 884744 | tf_op jit(solution)/shard_map/ppermute | solution.py:321
  100.1 3.8 %collective-permute-start.1 = (bf16[2,8,192,128]{3,2,1,0:T(8,128)(2,1)}, bf16[2,8,192,128]{3,2,1,0:T(8,128)(2,1)S(1)}, u32[]{:S(2)}, u32[]{:S(2)}) collective-permute-start(bf16[2,8,192,128]{3,2,1,0:T(8,128)(2,1)} %pad_maximum_fusion.pair_hbm), channel_id=1, source_target_pairs={{0,2},{1,7},{2,4},{3,1},{4,6},{5,3},{6,0},{7,5},{8,10},{9,15},{10,... | collective-permute-start | bytes 2359304 | tf_op jit(solution)/shard_map/ppermute | solution.py:300
  103.9 0.0 collective-permute-done.4
  103.9 0.0 copy-start.2
  103.9 0.0 collective-permute-done.5
  103.9 0.0 copy-start.3
  103.9 0.0 collective-permute-done.3.other_ref
  103.9 1.3 copy-done.2
  105.2 0.7 copy-done.3
  105.9 1.6 copy-done
  107.5 1.0 copy-done.1
  108.5 4.3 %shard_map.114 = bf16[4,192,512]{2,1,0:T(8,128)(2,1)} custom-call(s32[1]{0:T(128)S(6)} %and.4.core_ref, bf16[192,768]{1,0:T(8,128)(2,1)S(1)} %copy-done.1, bf16[192,768]{1,0:T(8,128)(2,1)S(1)} %collective-permute-done.3.other_ref, bf16[8,512,256]{2,1,0:T(8,128)(2,1)S(1)} %bitcast.21, bf16[8,512,256]{2,1,0:T(8,128)(2,1)} %bitcast.23, ...), custom_call_target="tpu_custom_call" | custom-call | flops 800000000 | bytes 6000000 | tf_op jit(solution)/shard_map/pallas_call | solution.py:323
  112.8 3.5 %all-to-all-start.2 = ((bf16[4,192,512]{2,1,0:T(8,128)(2,1)}), bf16[4,192,512]{2,1,0:T(8,128)(2,1)S(1)}, u32[]{:S(2)}, u32[]{:S(2)}) async-start(bf16[4,192,512]{2,1,0:T(8,128)(2,1)} %shard_map.114), calls=%async_computation.2 | async-start | bytes 1572864 | tf_op jit(solution)/shard_map/all_to_all | solution.py:332
  116.3 0.0 copy-done.5
  116.3 4.8 %collective-permute-start.2 = (bf16[8,192,128]{2,1,0:T(8,128)(2,1)S(1)}, bf16[8,192,128]{2,1,0:T(8,128)(2,1)S(1)}, u32[]{:S(2)}, u32[]{:S(2)}) collective-permute-start(bf16[8,192,128]{2,1,0:T(8,128)(2,1)S(1)} %copy-done.5), channel_id=1, source_target_pairs={{0,4},{1,5},{2,6},{3,7},{4,0},{5,1},{6,2},{7,3},{8,12},{9,13},{10,... | collective-permute-start | bytes 1179656 | tf_op jit(solution)/shard_map/ppermute | solution.py:301
  121.1 7.7 %all-to-all-done.2.parts_ref = bf16[4,192,512]{2,1,0:T(8,128)(2,1)S(1)} async-done(((bf16[4,192,512]{2,1,0:T(8,128)(2,1)}), bf16[4,192,512]{2,1,0:T(8,128)(2,1)S(1)}, u32[]{:S(2)}, u32[]{:S(2)}) %all-to-all-start.2) | async-done | bytes 786464 | tf_op jit(solution)/shard_map/all_to_all | solution.py:332
  128.9 0.9 shard_map.115
  129.8 7.5 %collective-permute-done.2.far_hbm = bf16[8,192,128]{2,1,0:T(8,128)(2,1)S(1)} collective-permute-done((bf16[8,192,128]{2,1,0:T(8,128)(2,1)S(1)}, bf16[8,192,128]{2,1,0:T(8,128)(2,1)S(1)}, u32[]{:S(2)}, u32[]{:S(2)}) %collective-permute-start.2) | collective-permute-done | bytes 393248 | tf_op jit(solution)/shard_map/ppermute | solution.py:301
  137.3 0.0 collective-permute-done.1.side_hbm
  137.3 0.9 copy-done.6
  138.2 2.5 %collective-permute-start.6 = (bf16[2,8,192,128]{3,2,1,0:T(8,128)(2,1)S(1)}, bf16[2,8,192,128]{3,2,1,0:T(8,128)(2,1)S(1)}, u32[]{:S(2)}, u32[]{:S(2)}) collective-permute-start(bf16[2,8,192,128]{3,2,1,0:T(8,128)(2,1)S(1)} %collective-permute-done.1.side_hbm), channel_id=1, source_target_pairs={{0,1},{1,0},{2,3},{3,2},{4,5},{5,4},{6,7},{7,6},{8,9},{9,8},{10,11... | collective-permute-start | bytes 2359304 | tf_op jit(solution)/shard_map/ppermute | solution.py:337
  140.8 12.3 %all-to-all-start.3 = ((bf16[16,24,256]{2,1,0:T(8,128)(2,1)}), bf16[16,24,256]{2,1,0:T(8,128)(2,1)}, u32[]{:S(2)}, u32[]{:S(2)}) async-start(bf16[16,24,256]{2,1,0:T(8,128)(2,1)} %shard_map.115), calls=%async_computation.3 | async-start | bytes 393216 | tf_op jit(solution)/shard_map/all_to_all | solution.py:339
  153.1 2.2 %collective-permute-start.7 = (bf16[8,192,128]{2,1,0:T(8,128)(2,1)S(1)}, bf16[8,192,128]{2,1,0:T(8,128)(2,1)S(1)}, u32[]{:S(2)}, u32[]{:S(2)}) collective-permute-start(bf16[8,192,128]{2,1,0:T(8,128)(2,1)S(1)} %collective-permute-done.2.far_hbm), channel_id=1, source_target_pairs={{0,1},{1,0},{2,3},{3,2},{4,5},{5,4},{6,7},{7,6},{8,9},{9,8},{10,11... | collective-permute-start | bytes 1179656 | tf_op jit(solution)/shard_map/ppermute | solution.py:338
  155.3 1.4 collective-permute-done.7.far2_hbm
  156.7 0.0 collective-permute-done.6.side2_hbm
  156.7 0.0 copy-done.8
  156.7 0.8 copy-done.9
  157.5 0.9 copy-done.7
  158.4 5.7 %shard_map.116 = (bf16[512,256]{1,0:T(8,128)(2,1)}, bf16[512,256]{1,0:T(8,128)(2,1)}, bf16[256,512]{1,0:T(8,128)(2,1)}) custom-call(s32[1]{0:T(128)} %bitcast.2.t_ref, bf16[1536,768]{1,0:T(8,128)(2,1)} %all-gather.5.cloned.1.call-done.delta_ref, bf16[2,8,192,128]{3,2,1,0:T(8,128)(2,1)} %pad_maximum_fusion.pair_hbm, bf16[2,8,192,128]{3,2,1,0:T(8,128)(2,1)} %copy-done.6, ...), custom_call_target="tpu_custom_call" | custom-call | flops 1200000000 | bytes 6000000 | tf_op jit(solution)/shard_map/pallas_call | solution.py:340
  164.1 2.3 %all-to-all-done.3 = bf16[16,24,256]{2,1,0:T(8,128)(2,1)} async-done(((bf16[16,24,256]{2,1,0:T(8,128)(2,1)}), bf16[16,24,256]{2,1,0:T(8,128)(2,1)}, u32[]{:S(2)}, u32[]{:S(2)}) %all-to-all-start.3) | async-done | bytes 196640 | tf_op jit(solution)/shard_map/all_to_all | solution.py:339
  166.4 1.9 %shard_map.117 = bf16[128,512]{1,0:T(8,128)(2,1)} custom-call(s32[2,128]{1,0:T(2,128)} %bitcast.33, s32[2,128]{1,0:T(2,128)} %bitcast.35, bf16[384,256]{1,0:T(8,128)(2,1)} %bitcast.16.ret_ref), custom_call_target="tpu_custom_call" | custom-call | flops 50000000 | bytes 400000 | tf_op jit(solution)/shard_map/pallas_call | solution.py:349
  (8 shorter events, 0.0 us)
Async XLA Ops:
  7.2 80.2 %all-gather.3.cloned.1.call-start = ((), (), s32[]{:S(2)}) async-start(), calls=%async_computation.4 | async-start | bytes 3538944 | tf_op jit(solution)/shard_map/all_gather | solution.py:292
  47.6 110.8 %all-gather.5.cloned.1.call-start = ((), (), s32[]{:S(2)}) async-start(), calls=%async_computation.5 | async-start | bytes 2654208 | tf_op jit(solution)/shard_map/all_gather | solution.py:319
  67.1 11.5 %copy-start.4 = (bf16[8,192,128]{2,1,0:T(8,128)(2,1)}, bf16[8,192,128]{2,1,0:T(8,128)(2,1)S(1)}, u32[]{:S(2)}) copy-start(bf16[8,192,128]{2,1,0:T(8,128)(2,1)S(1)} %all_to_all.21) | copy-start | bytes 1179652
  67.1 11.4 %collective-permute-start = (bf16[8,192,128]{2,1,0:T(8,128)(2,1)S(1)}, bf16[8,192,128]{2,1,0:T(8,128)(2,1)S(1)}, u32[]{:S(2)}, u32[]{:S(2)}) collective-permute-start(bf16[8,192,128]{2,1,0:T(8,128)(2,1)S(1)} %all_to_all.21), channel_id=1, source_target_pairs={{0,1},{1,0},{2,3},{3,2},{4,5},{5,4},{6,7},{7,6},{8,9},{9,8},{10,11... | collective-permute-start | bytes 1179656 | tf_op jit(solution)/shard_map/ppermute | solution.py:298
  93.6 10.3 %collective-permute-start.4 = (bf16[1,4096,256]{2,1,0:T(8,128)(2,1)}, bf16[1,4096,256]{2,1,0:T(8,128)(2,1)S(1)}, u32[]{:S(2)}, u32[]{:S(2)}) collective-permute-start(bf16[1,4096,256]{2,1,0:T(8,128)(2,1)} %param.13), channel_id=1, source_target_pairs={{0,1},{1,0},{2,3},{3,2},{4,5},{5,4},{6,7},{7,6},{8,9},{9,8},{10,11... | collective-permute-start | bytes 6291464 | tf_op jit(solution)/shard_map/ppermute | solution.py:302
  95.8 8.1 %collective-permute-start.5 = (bf16[1,4096,256]{2,1,0:T(8,128)(2,1)}, bf16[1,4096,256]{2,1,0:T(8,128)(2,1)S(1)}, u32[]{:S(2)}, u32[]{:S(2)}) collective-permute-start(bf16[1,4096,256]{2,1,0:T(8,128)(2,1)} %param.14), channel_id=1, source_target_pairs={{0,1},{1,0},{2,3},{3,2},{4,5},{5,4},{6,7},{7,6},{8,9},{9,8},{10,11... | collective-permute-start | bytes 6291464 | tf_op jit(solution)/shard_map/ppermute | solution.py:303
  97.9 6.0 %collective-permute-start.3 = (bf16[192,768]{1,0:T(8,128)(2,1)}, bf16[192,768]{1,0:T(8,128)(2,1)S(1)}, u32[]{:S(2)}, u32[]{:S(2)}) collective-permute-start(bf16[192,768]{1,0:T(8,128)(2,1)} %shard_map.113.own_ref), channel_id=1, source_target_pairs={{0,1},{1,0},{2,3},{3,2},{4,5},{5,4},{6,7},{7,6},{8,9},{9,8},{10,11... | collective-permute-start | bytes 884744 | tf_op jit(solution)/shard_map/ppermute | solution.py:321
  100.1 37.2 %collective-permute-start.1 = (bf16[2,8,192,128]{3,2,1,0:T(8,128)(2,1)}, bf16[2,8,192,128]{3,2,1,0:T(8,128)(2,1)S(1)}, u32[]{:S(2)}, u32[]{:S(2)}) collective-permute-start(bf16[2,8,192,128]{3,2,1,0:T(8,128)(2,1)} %pad_maximum_fusion.pair_hbm), channel_id=1, source_target_pairs={{0,2},{1,7},{2,4},{3,1},{4,6},{5,3},{6,0},{7,5},{8,10},{9,15},{10,... | collective-permute-start | bytes 2359304 | tf_op jit(solution)/shard_map/ppermute | solution.py:300
  103.9 1.3 copy-start.2
  103.9 2.0 %copy-start.3 = (bf16[1,4096,256]{2,1,0:T(8,128)(2,1)}, bf16[1,4096,256]{2,1,0:T(8,128)(2,1)S(1)}, u32[]{:S(2)}) copy-start(bf16[1,4096,256]{2,1,0:T(8,128)(2,1)S(1)} %collective-permute-done.5) | copy-start | bytes 6291460
  105.9 1.6 copy-start
  107.5 1.0 copy-start.1
  108.5 7.8 %copy-start.5 = (bf16[8,192,128]{2,1,0:T(8,128)(2,1)S(1)}, bf16[8,192,128]{2,1,0:T(8,128)(2,1)}, u32[]{:S(2)}) copy-start(bf16[8,192,128]{2,1,0:T(8,128)(2,1)} %copy-done.4) | copy-start | bytes 1179652
  112.8 16.1 %all-to-all-start.2 = ((bf16[4,192,512]{2,1,0:T(8,128)(2,1)}), bf16[4,192,512]{2,1,0:T(8,128)(2,1)S(1)}, u32[]{:S(2)}, u32[]{:S(2)}) async-start(bf16[4,192,512]{2,1,0:T(8,128)(2,1)} %shard_map.114), calls=%async_computation.2 | async-start | bytes 1572864 | tf_op jit(solution)/shard_map/all_to_all | solution.py:332
  116.3 21.0 %collective-permute-start.2 = (bf16[8,192,128]{2,1,0:T(8,128)(2,1)S(1)}, bf16[8,192,128]{2,1,0:T(8,128)(2,1)S(1)}, u32[]{:S(2)}, u32[]{:S(2)}) collective-permute-start(bf16[8,192,128]{2,1,0:T(8,128)(2,1)S(1)} %copy-done.5), channel_id=1, source_target_pairs={{0,4},{1,5},{2,6},{3,7},{4,0},{5,1},{6,2},{7,3},{8,12},{9,13},{10,... | collective-permute-start | bytes 1179656 | tf_op jit(solution)/shard_map/ppermute | solution.py:301
  137.3 19.4 %copy-start.8 = (bf16[8,192,128]{2,1,0:T(8,128)(2,1)}, bf16[8,192,128]{2,1,0:T(8,128)(2,1)S(1)}, u32[]{:S(2)}) copy-start(bf16[8,192,128]{2,1,0:T(8,128)(2,1)S(1)} %collective-permute-done.2.far_hbm) | copy-start | bytes 1179652
  137.3 0.9 copy-start.6
  138.2 18.5 %collective-permute-start.6 = (bf16[2,8,192,128]{3,2,1,0:T(8,128)(2,1)S(1)}, bf16[2,8,192,128]{3,2,1,0:T(8,128)(2,1)S(1)}, u32[]{:S(2)}, u32[]{:S(2)}) collective-permute-start(bf16[2,8,192,128]{3,2,1,0:T(8,128)(2,1)S(1)} %collective-permute-done.1.side_hbm), channel_id=1, source_target_pairs={{0,1},{1,0},{2,3},{3,2},{4,5},{5,4},{6,7},{7,6},{8,9},{9,8},{10,11... | collective-permute-start | bytes 2359304 | tf_op jit(solution)/shard_map/ppermute | solution.py:337
  140.8 25.6 %all-to-all-start.3 = ((bf16[16,24,256]{2,1,0:T(8,128)(2,1)}), bf16[16,24,256]{2,1,0:T(8,128)(2,1)}, u32[]{:S(2)}, u32[]{:S(2)}) async-start(bf16[16,24,256]{2,1,0:T(8,128)(2,1)} %shard_map.115), calls=%async_computation.3 | async-start | bytes 393216 | tf_op jit(solution)/shard_map/all_to_all | solution.py:339
  153.1 3.6 %collective-permute-start.7 = (bf16[8,192,128]{2,1,0:T(8,128)(2,1)S(1)}, bf16[8,192,128]{2,1,0:T(8,128)(2,1)S(1)}, u32[]{:S(2)}, u32[]{:S(2)}) collective-permute-start(bf16[8,192,128]{2,1,0:T(8,128)(2,1)S(1)} %collective-permute-done.2.far_hbm), channel_id=1, source_target_pairs={{0,1},{1,0},{2,3},{3,2},{4,5},{5,4},{6,7},{7,6},{8,9},{9,8},{10,11... | collective-permute-start | bytes 1179656 | tf_op jit(solution)/shard_map/ppermute | solution.py:338
  156.7 0.8 copy-start.9
  157.5 0.9 copy-start.7
Sparse Core Ops, SparseCore 0:
  47.7 39.5 all-gather.2
  93.7 45.1 all-gather.4

commit v5 on v4

--- a/solution.py
+++ b/solution.py
@@ -219,7 +219,7 @@
             out_ref[q * 4 + j] = x[:, j * 128 : (j + 1) * 128]
 
 
-def weight_kernel(t_ref, delta_ref, pair_hbm, side_hbm, side2_hbm, far_hbm, far2_hbm, gate_ref, up_ref, down_ref, buf, sem):
+def weight_kernel(t_ref, delta_hbm, pair_hbm, side_hbm, side2_hbm, far_hbm, far2_hbm, gate_ref, up_ref, down_ref, buf, delta_ref, sem):
     t = t_ref[0]
     core = lax.rem(t, 2)
     chip = lax.div(t, 2)
@@ -238,6 +238,7 @@
         pltpu.make_async_copy(src, buf.at[lax.rem(chip + shift, 4) * 2 + which], sem.at[i])
         for i, (src, shift, which) in enumerate(places)
     ]
+    copies.append(pltpu.make_async_copy(delta_hbm, delta_ref, sem.at[8]))
     for copy in copies:
         copy.start()
     for copy in copies:
@@ -340,8 +341,8 @@
     gate_grad, up_grad, down_grad = call(
         weight_kernel,
         [shape((512, 256)), shape((512, 256)), shape((256, 512))],
-        [SM, VM, HB, HB, HB, HB, HB],
-        [pltpu.VMEM((8, 8, 192, 128), BF), dma((8,))],
+        [SM, HB, HB, HB, HB, HB, HB],
+        [pltpu.VMEM((8, 8, 192, 128), BF), pltpu.VMEM((1536, 768), BF), dma((9,))],
         flops=1_200_000_000,
         size=6_000_000,
     )(t, deltas, pair, side, side2, far, far2)

time: 178 us -> 178 us (level)
  no operation moved by 1% of the time
where the time goes in v5:
time: 178 us; the launch traced here: 175 us
  blocking collectives  55.2 us (31%)
  starting transfers between devices  45.7 us (26%)
  waiting for transfers between devices  29.2 us (16%)
  Pallas kernels  22.7 us (13%)
  between operations  14.2 us (8%)
  local copies, waits for them, and re-layouts  7.15 us (4%)
    all_to_all x1, blocking collectives, layer(): lax.all_to_all(sent.reshape(16, 24, 512), 'expert', 0, 0, tiled=True)  37.6 us
    all_to_all x1, blocking collectives, layer(): mine = lax.all_to_all(corner, 'dp', 0, 0, tiled=True)  17.6 us
    all_to_all x1, starting transfers between devices, layer(): returned = lax.all_to_all(back, 'expert', 0, 0, tiled=True)  12.3 us
    ppermute x1, starting transfers between devices, layer(): turned = lax.ppermute(mine, 'tensor', SWAP)  9.97 us
    all_gather x1, waiting for transfers between devices, layer(): lax.all_gather(block.reshape(384, 512), 'tensor', axis=0, tiled=True)  7.83 us
    all_to_all x1, waiting for transfers between devices, layer(): lax.all_to_all(terms, 'tensor', 0, 0, axis_index_groups=[[0, 2, 4, 6], [1...  7.73 us
    ppermute x1, waiting for transfers between devices, layer(): far = lax.ppermute(mine, 'tensor', FAR)  7.52 us
    unnamed x20, local copies, waits for them, and re-layouts  7.15 us
  transfers between devices with their start and end apart: 12, of which 6 were waited for; matrix products, arithmetic and copies ran while one was open for 1% of the time, Pallas kernels for 7%

profile of v5, /device:TPU:1, one launch (start us, length us, event | category | flops | bytes accessed | tf_op | source)
XLA Modules:
  0.0 175.1 jit_solution(15747139714675363803)
XLA Ops:
  7.2 0.0 all-gather.3.cloned.1.call-start
  7.2 2.7 %shard_map.111 = bf16[384,512]{1,0:T(8,128)(2,1)} custom-call(s32[1]{0:T(128)} %bitcast.2.t_ref, s32[2,128]{1,0:T(2,128)} %bitcast.32, s32[2,128]{1,0:T(2,128)} %bitcast.34, f32[2,128]{1,0:T(2,128)} %bitcast.36, bf16[128,4096]{1,0:T(8,128)(2,1)} %tok_hbm.1, bf16[128,4096]{1,0:T(8,128)(2,1)} %grad_hbm.1), custom_call_target="tpu_custom_call" | custom-call | flops 100000000 | bytes 700000 | tf_op jit(solution)/shard_map/pallas_call | solution.py:284
  10.0 37.6 %all_to_all.20.block_ref = bf16[16,24,512]{2,1,0:T(8,128)(2,1)} all-to-all(bf16[16,24,512]{2,1,0:T(8,128)(2,1)} %bitcast.30), channel_id=1, replica_groups=mesh['expert'=16,'dp'=8,'tensor'=8] {'expert'}, dimensions={0} | all-to-all | bytes 786432 | tf_op jit(solution)/shard_map/all_to_all | solution.py:292
  47.6 0.0 all-gather.3.cloned.1.call-update
  47.6 0.0 all-gather.5.cloned.1.call-start
  47.7 1.9 %shard_map.112 = bf16[8,192,128]{2,1,0:T(8,128)(2,1)} custom-call(bf16[16,24,512]{2,1,0:T(8,128)(2,1)} %all_to_all.20.block_ref), custom_call_target="tpu_custom_call" | custom-call | flops 20000000 | bytes 800000 | tf_op jit(solution)/shard_map/pallas_call | solution.py:295
  49.6 17.6 %all_to_all.21 = bf16[8,192,128]{2,1,0:T(8,128)(2,1)S(1)} all-to-all(bf16[8,192,128]{2,1,0:T(8,128)(2,1)} %shard_map.112), channel_id=1, replica_groups=mesh['expert'=16,'dp'=8,'tensor'=8] {'dp'}, dimensions={0} | all-to-all | bytes 786432 | tf_op jit(solution)/shard_map/all_to_all | solution.py:298
  67.1 0.0 copy-start.4
  67.1 10.0 %collective-permute-start = (bf16[8,192,128]{2,1,0:T(8,128)(2,1)S(1)}, bf16[8,192,128]{2,1,0:T(8,128)(2,1)S(1)}, u32[]{:S(2)}, u32[]{:S(2)}) collective-permute-start(bf16[8,192,128]{2,1,0:T(8,128)(2,1)S(1)} %all_to_all.21), channel_id=1, source_target_pairs={{0,1},{1,0},{2,3},{3,2},{4,5},{5,4},{6,7},{7,6},{8,9},{9,8},{10,11... | collective-permute-start | bytes 1179656 | tf_op jit(solution)/shard_map/ppermute | solution.py:299
  77.1 1.5 collective-permute-done
  78.6 0.0 copy-done.4
  78.6 0.9 pad_maximum_fusion.pair_hbm
  79.5 7.8 %all-gather.3.cloned.1.call-done = bf16[3072,512]{1,0:T(8,128)(2,1)} async-done(((bf16[384,512]{1,0:T(8,128)(2,1)}), bf16[3072,512]{1,0:T(8,128)(2,1)}) %all-gather.3.cloned.1.call-update) | async-done | bytes 3145744 | tf_op jit(solution)/shard_map/all_gather | solution.py:293
  87.4 6.2 %shard_map.113.own_ref = bf16[192,768]{1,0:T(8,128)(2,1)} custom-call(bf16[8,16,24,512]{3,2,1,0:T(8,128)(2,1)} %bitcast.25, bf16[8,4,128,256]{3,2,1,0:T(8,128)(2,1)} %bitcast.20, bf16[8,4,128,256]{3,2,1,0:T(8,128)(2,1)} %bitcast.22, bf16[256,4096]{1,0:T(8,128)(2,1)} %bitcast.26), custom_call_target="tpu_custom_call" | custom-call | flops 1300000000 | bytes 10000000 | tf_op jit(solution)/shard_map/pallas_call | solution.py:307
  93.5 0.0 all-gather.5.cloned.1.call-update
  93.6 2.2 %collective-permute-start.4 = (bf16[1,4096,256]{2,1,0:T(8,128)(2,1)}, bf16[1,4096,256]{2,1,0:T(8,128)(2,1)S(1)}, u32[]{:S(2)}, u32[]{:S(2)}) collective-permute-start(bf16[1,4096,256]{2,1,0:T(8,128)(2,1)} %param.13), channel_id=1, source_target_pairs={{0,1},{1,0},{2,3},{3,2},{4,5},{5,4},{6,7},{7,6},{8,9},{9,8},{10,11... | collective-permute-start | bytes 6291464 | tf_op jit(solution)/shard_map/ppermute | solution.py:303
  95.8 2.1 %collective-permute-start.5 = (bf16[1,4096,256]{2,1,0:T(8,128)(2,1)}, bf16[1,4096,256]{2,1,0:T(8,128)(2,1)S(1)}, u32[]{:S(2)}, u32[]{:S(2)}) collective-permute-start(bf16[1,4096,256]{2,1,0:T(8,128)(2,1)} %param.14), channel_id=1, source_target_pairs={{0,1},{1,0},{2,3},{3,2},{4,5},{5,4},{6,7},{7,6},{8,9},{9,8},{10,11... | collective-permute-start | bytes 6291464 | tf_op jit(solution)/shard_map/ppermute | solution.py:304
  97.9 2.2 %collective-permute-start.3 = (bf16[192,768]{1,0:T(8,128)(2,1)}, bf16[192,768]{1,0:T(8,128)(2,1)S(1)}, u32[]{:S(2)}, u32[]{:S(2)}) collective-permute-start(bf16[192,768]{1,0:T(8,128)(2,1)} %shard_map.113.own_ref), channel_id=1, source_target_pairs={{0,1},{1,0},{2,3},{3,2},{4,5},{5,4},{6,7},{7,6},{8,9},{9,8},{10,11... | collective-permute-start | bytes 884744 | tf_op jit(solution)/shard_map/ppermute | solution.py:322
  100.1 3.8 %collective-permute-start.1 = (bf16[2,8,192,128]{3,2,1,0:T(8,128)(2,1)}, bf16[2,8,192,128]{3,2,1,0:T(8,128)(2,1)S(1)}, u32[]{:S(2)}, u32[]{:S(2)}) collective-permute-start(bf16[2,8,192,128]{3,2,1,0:T(8,128)(2,1)} %pad_maximum_fusion.pair_hbm), channel_id=1, source_target_pairs={{0,2},{1,7},{2,4},{3,1},{4,6},{5,3},{6,0},{7,5},{8,10},{9,15},{10,... | collective-permute-start | bytes 2359304 | tf_op jit(solution)/shard_map/ppermute | solution.py:301
  103.9 0.0 collective-permute-done.4
  103.9 0.0 copy-start.2
  103.9 0.0 collective-permute-done.5
  103.9 0.0 copy-start.3
  103.9 0.0 collective-permute-done.3.other_ref
  103.9 1.3 copy-done.2
  105.2 0.7 copy-done.3
  105.9 1.6 copy-done
  107.5 1.0 copy-done.1
  108.5 4.3 %shard_map.114 = bf16[4,192,512]{2,1,0:T(8,128)(2,1)} custom-call(s32[1]{0:T(128)S(6)} %and.4.core_ref, bf16[192,768]{1,0:T(8,128)(2,1)S(1)} %copy-done.1, bf16[192,768]{1,0:T(8,128)(2,1)S(1)} %collective-permute-done.3.other_ref, bf16[8,512,256]{2,1,0:T(8,128)(2,1)S(1)} %bitcast.21, bf16[8,512,256]{2,1,0:T(8,128)(2,1)} %bitcast.23, ...), custom_call_target="tpu_custom_call" | custom-call | flops 800000000 | bytes 6000000 | tf_op jit(solution)/shard_map/pallas_call | solution.py:324
  112.8 3.5 %all-to-all-start.2 = ((bf16[4,192,512]{2,1,0:T(8,128)(2,1)}), bf16[4,192,512]{2,1,0:T(8,128)(2,1)S(1)}, u32[]{:S(2)}, u32[]{:S(2)}) async-start(bf16[4,192,512]{2,1,0:T(8,128)(2,1)} %shard_map.114), calls=%async_computation.2 | async-start | bytes 1572864 | tf_op jit(solution)/shard_map/all_to_all | solution.py:333
  116.3 0.0 copy-done.5
  116.3 4.8 %collective-permute-start.2 = (bf16[8,192,128]{2,1,0:T(8,128)(2,1)S(1)}, bf16[8,192,128]{2,1,0:T(8,128)(2,1)S(1)}, u32[]{:S(2)}, u32[]{:S(2)}) collective-permute-start(bf16[8,192,128]{2,1,0:T(8,128)(2,1)S(1)} %copy-done.5), channel_id=1, source_target_pairs={{0,4},{1,5},{2,6},{3,7},{4,0},{5,1},{6,2},{7,3},{8,12},{9,13},{10,... | collective-permute-start | bytes 1179656 | tf_op jit(solution)/shard_map/ppermute | solution.py:302
  121.1 7.7 %all-to-all-done.2.parts_ref = bf16[4,192,512]{2,1,0:T(8,128)(2,1)S(1)} async-done(((bf16[4,192,512]{2,1,0:T(8,128)(2,1)}), bf16[4,192,512]{2,1,0:T(8,128)(2,1)S(1)}, u32[]{:S(2)}, u32[]{:S(2)}) %all-to-all-start.2) | async-done | bytes 786464 | tf_op jit(solution)/shard_map/all_to_all | solution.py:333
  128.9 0.9 shard_map.115
  129.8 7.5 %collective-permute-done.2.far_hbm = bf16[8,192,128]{2,1,0:T(8,128)(2,1)S(1)} collective-permute-done((bf16[8,192,128]{2,1,0:T(8,128)(2,1)S(1)}, bf16[8,192,128]{2,1,0:T(8,128)(2,1)S(1)}, u32[]{:S(2)}, u32[]{:S(2)}) %collective-permute-start.2) | collective-permute-done | bytes 393248 | tf_op jit(solution)/shard_map/ppermute | solution.py:302
  137.3 0.0 collective-permute-done.1.side_hbm
  137.3 0.9 copy-done.6
  138.2 2.5 %collective-permute-start.6 = (bf16[2,8,192,128]{3,2,1,0:T(8,128)(2,1)S(1)}, bf16[2,8,192,128]{3,2,1,0:T(8,128)(2,1)S(1)}, u32[]{:S(2)}, u32[]{:S(2)}) collective-permute-start(bf16[2,8,192,128]{3,2,1,0:T(8,128)(2,1)S(1)} %collective-permute-done.1.side_hbm), channel_id=1, source_target_pairs={{0,1},{1,0},{2,3},{3,2},{4,5},{5,4},{6,7},{7,6},{8,9},{9,8},{10,11... | collective-permute-start | bytes 2359304 | tf_op jit(solution)/shard_map/ppermute | solution.py:338
  140.8 12.3 %all-to-all-start.3 = ((bf16[16,24,256]{2,1,0:T(8,128)(2,1)}), bf16[16,24,256]{2,1,0:T(8,128)(2,1)}, u32[]{:S(2)}, u32[]{:S(2)}) async-start(bf16[16,24,256]{2,1,0:T(8,128)(2,1)} %shard_map.115), calls=%async_computation.3 | async-start | bytes 393216 | tf_op jit(solution)/shard_map/all_to_all | solution.py:340
  153.1 2.2 %collective-permute-start.7 = (bf16[8,192,128]{2,1,0:T(8,128)(2,1)S(1)}, bf16[8,192,128]{2,1,0:T(8,128)(2,1)S(1)}, u32[]{:S(2)}, u32[]{:S(2)}) collective-permute-start(bf16[8,192,128]{2,1,0:T(8,128)(2,1)S(1)} %collective-permute-done.2.far_hbm), channel_id=1, source_target_pairs={{0,1},{1,0},{2,3},{3,2},{4,5},{5,4},{6,7},{7,6},{8,9},{9,8},{10,11... | collective-permute-start | bytes 1179656 | tf_op jit(solution)/shard_map/ppermute | solution.py:339
  155.3 1.4 collective-permute-done.7.far2_hbm
  156.7 0.0 collective-permute-done.6.side2_hbm
  156.7 0.0 copy-done.8
  156.7 0.8 copy-done.9
  157.5 0.9 copy-done.7
  158.4 4.8 %shard_map.116 = (bf16[512,256]{1,0:T(8,128)(2,1)}, bf16[512,256]{1,0:T(8,128)(2,1)}, bf16[256,512]{1,0:T(8,128)(2,1)}) custom-call(s32[1]{0:T(128)} %bitcast.2.t_ref, bf16[1536,768]{1,0:T(8,128)(2,1)} %all-gather.5.cloned.1.call-done.delta_hbm, bf16[2,8,192,128]{3,2,1,0:T(8,128)(2,1)} %pad_maximum_fusion.pair_hbm, bf16[2,8,192,128]{3,2,1,0:T(8,128)(2,1)} %copy-done.6, ...), custom_call_target="tpu_custom_call" | custom-call | flops 1200000000 | bytes 6000000 | tf_op jit(solution)/shard_map/pallas_call | solution.py:341
  163.2 3.2 %all-to-all-done.3 = bf16[16,24,256]{2,1,0:T(8,128)(2,1)} async-done(((bf16[16,24,256]{2,1,0:T(8,128)(2,1)}), bf16[16,24,256]{2,1,0:T(8,128)(2,1)}, u32[]{:S(2)}, u32[]{:S(2)}) %all-to-all-start.3) | async-done | bytes 196640 | tf_op jit(solution)/shard_map/all_to_all | solution.py:340
  166.4 1.9 %shard_map.117 = bf16[128,512]{1,0:T(8,128)(2,1)} custom-call(s32[2,128]{1,0:T(2,128)} %bitcast.33, s32[2,128]{1,0:T(2,128)} %bitcast.35, bf16[384,256]{1,0:T(8,128)(2,1)} %bitcast.16.ret_ref), custom_call_target="tpu_custom_call" | custom-call | flops 50000000 | bytes 400000 | tf_op jit(solution)/shard_map/pallas_call | solution.py:350
  (8 shorter events, 0.0 us)
Async XLA Ops:
  7.2 80.2 %all-gather.3.cloned.1.call-start = ((), (), s32[]{:S(2)}) async-start(), calls=%async_computation.4 | async-start | bytes 3538944 | tf_op jit(solution)/shard_map/all_gather | solution.py:293
  47.6 110.8 %all-gather.5.cloned.1.call-start = ((), (), s32[]{:S(2)}) async-start(), calls=%async_computation.5 | async-start | bytes 2654208 | tf_op jit(solution)/shard_map/all_gather | solution.py:320
  67.1 11.5 %copy-start.4 = (bf16[8,192,128]{2,1,0:T(8,128)(2,1)}, bf16[8,192,128]{2,1,0:T(8,128)(2,1)S(1)}, u32[]{:S(2)}) copy-start(bf16[8,192,128]{2,1,0:T(8,128)(2,1)S(1)} %all_to_all.21) | copy-start | bytes 1179652
  67.1 11.4 %collective-permute-start = (bf16[8,192,128]{2,1,0:T(8,128)(2,1)S(1)}, bf16[8,192,128]{2,1,0:T(8,128)(2,1)S(1)}, u32[]{:S(2)}, u32[]{:S(2)}) collective-permute-start(bf16[8,192,128]{2,1,0:T(8,128)(2,1)S(1)} %all_to_all.21), channel_id=1, source_target_pairs={{0,1},{1,0},{2,3},{3,2},{4,5},{5,4},{6,7},{7,6},{8,9},{9,8},{10,11... | collective-permute-start | bytes 1179656 | tf_op jit(solution)/shard_map/ppermute | solution.py:299
  93.6 10.3 %collective-permute-start.4 = (bf16[1,4096,256]{2,1,0:T(8,128)(2,1)}, bf16[1,4096,256]{2,1,0:T(8,128)(2,1)S(1)}, u32[]{:S(2)}, u32[]{:S(2)}) collective-permute-start(bf16[1,4096,256]{2,1,0:T(8,128)(2,1)} %param.13), channel_id=1, source_target_pairs={{0,1},{1,0},{2,3},{3,2},{4,5},{5,4},{6,7},{7,6},{8,9},{9,8},{10,11... | collective-permute-start | bytes 6291464 | tf_op jit(solution)/shard_map/ppermute | solution.py:303
  95.8 8.1 %collective-permute-start.5 = (bf16[1,4096,256]{2,1,0:T(8,128)(2,1)}, bf16[1,4096,256]{2,1,0:T(8,128)(2,1)S(1)}, u32[]{:S(2)}, u32[]{:S(2)}) collective-permute-start(bf16[1,4096,256]{2,1,0:T(8,128)(2,1)} %param.14), channel_id=1, source_target_pairs={{0,1},{1,0},{2,3},{3,2},{4,5},{5,4},{6,7},{7,6},{8,9},{9,8},{10,11... | collective-permute-start | bytes 6291464 | tf_op jit(solution)/shard_map/ppermute | solution.py:304
  97.9 6.0 %collective-permute-start.3 = (bf16[192,768]{1,0:T(8,128)(2,1)}, bf16[192,768]{1,0:T(8,128)(2,1)S(1)}, u32[]{:S(2)}, u32[]{:S(2)}) collective-permute-start(bf16[192,768]{1,0:T(8,128)(2,1)} %shard_map.113.own_ref), channel_id=1, source_target_pairs={{0,1},{1,0},{2,3},{3,2},{4,5},{5,4},{6,7},{7,6},{8,9},{9,8},{10,11... | collective-permute-start | bytes 884744 | tf_op jit(solution)/shard_map/ppermute | solution.py:322
  100.1 37.2 %collective-permute-start.1 = (bf16[2,8,192,128]{3,2,1,0:T(8,128)(2,1)}, bf16[2,8,192,128]{3,2,1,0:T(8,128)(2,1)S(1)}, u32[]{:S(2)}, u32[]{:S(2)}) collective-permute-start(bf16[2,8,192,128]{3,2,1,0:T(8,128)(2,1)} %pad_maximum_fusion.pair_hbm), channel_id=1, source_target_pairs={{0,2},{1,7},{2,4},{3,1},{4,6},{5,3},{6,0},{7,5},{8,10},{9,15},{10,... | collective-permute-start | bytes 2359304 | tf_op jit(solution)/shard_map/ppermute | solution.py:301
  103.9 1.3 copy-start.2
  103.9 2.0 %copy-start.3 = (bf16[1,4096,256]{2,1,0:T(8,128)(2,1)}, bf16[1,4096,256]{2,1,0:T(8,128)(2,1)S(1)}, u32[]{:S(2)}) copy-start(bf16[1,4096,256]{2,1,0:T(8,128)(2,1)S(1)} %collective-permute-done.5) | copy-start | bytes 6291460
  105.9 1.6 copy-start
  107.5 1.0 copy-start.1
  108.5 7.8 %copy-start.5 = (bf16[8,192,128]{2,1,0:T(8,128)(2,1)S(1)}, bf16[8,192,128]{2,1,0:T(8,128)(2,1)}, u32[]{:S(2)}) copy-start(bf16[8,192,128]{2,1,0:T(8,128)(2,1)} %copy-done.4) | copy-start | bytes 1179652
  112.8 16.1 %all-to-all-start.2 = ((bf16[4,192,512]{2,1,0:T(8,128)(2,1)}), bf16[4,192,512]{2,1,0:T(8,128)(2,1)S(1)}, u32[]{:S(2)}, u32[]{:S(2)}) async-start(bf16[4,192,512]{2,1,0:T(8,128)(2,1)} %shard_map.114), calls=%async_computation.2 | async-start | bytes 1572864 | tf_op jit(solution)/shard_map/all_to_all | solution.py:333
  116.3 21.0 %collective-permute-start.2 = (bf16[8,192,128]{2,1,0:T(8,128)(2,1)S(1)}, bf16[8,192,128]{2,1,0:T(8,128)(2,1)S(1)}, u32[]{:S(2)}, u32[]{:S(2)}) collective-permute-start(bf16[8,192,128]{2,1,0:T(8,128)(2,1)S(1)} %copy-done.5), channel_id=1, source_target_pairs={{0,4},{1,5},{2,6},{3,7},{4,0},{5,1},{6,2},{7,3},{8,12},{9,13},{10,... | collective-permute-start | bytes 1179656 | tf_op jit(solution)/shard_map/ppermute | solution.py:302
  137.3 19.4 %copy-start.8 = (bf16[8,192,128]{2,1,0:T(8,128)(2,1)}, bf16[8,192,128]{2,1,0:T(8,128)(2,1)S(1)}, u32[]{:S(2)}) copy-start(bf16[8,192,128]{2,1,0:T(8,128)(2,1)S(1)} %collective-permute-done.2.far_hbm) | copy-start | bytes 1179652
  137.3 0.9 copy-start.6
  138.2 18.5 %collective-permute-start.6 = (bf16[2,8,192,128]{3,2,1,0:T(8,128)(2,1)S(1)}, bf16[2,8,192,128]{3,2,1,0:T(8,128)(2,1)S(1)}, u32[]{:S(2)}, u32[]{:S(2)}) collective-permute-start(bf16[2,8,192,128]{3,2,1,0:T(8,128)(2,1)S(1)} %collective-permute-done.1.side_hbm), channel_id=1, source_target_pairs={{0,1},{1,0},{2,3},{3,2},{4,5},{5,4},{6,7},{7,6},{8,9},{9,8},{10,11... | collective-permute-start | bytes 2359304 | tf_op jit(solution)/shard_map/ppermute | solution.py:338
  140.8 25.6 %all-to-all-start.3 = ((bf16[16,24,256]{2,1,0:T(8,128)(2,1)}), bf16[16,24,256]{2,1,0:T(8,128)(2,1)}, u32[]{:S(2)}, u32[]{:S(2)}) async-start(bf16[16,24,256]{2,1,0:T(8,128)(2,1)} %shard_map.115), calls=%async_computation.3 | async-start | bytes 393216 | tf_op jit(solution)/shard_map/all_to_all | solution.py:340
  153.1 3.6 %collective-permute-start.7 = (bf16[8,192,128]{2,1,0:T(8,128)(2,1)S(1)}, bf16[8,192,128]{2,1,0:T(8,128)(2,1)S(1)}, u32[]{:S(2)}, u32[]{:S(2)}) collective-permute-start(bf16[8,192,128]{2,1,0:T(8,128)(2,1)S(1)} %collective-permute-done.2.far_hbm), channel_id=1, source_target_pairs={{0,1},{1,0},{2,3},{3,2},{4,5},{5,4},{6,7},{7,6},{8,9},{9,8},{10,11... | collective-permute-start | bytes 1179656 | tf_op jit(solution)/shard_map/ppermute | solution.py:339
  156.7 0.8 copy-start.9
  157.5 0.9 copy-start.7
Sparse Core Ops, SparseCore 0:
  47.7 39.5 all-gather.2
  93.7 45.1 all-gather.4
